TPU v7x, 32 devices: a whole 2x2x4 slice. The times are simulated.
32 devices in a mesh: groups: 2 (over y), space: 4 (over z), phase: 4 (over x, core).
Axes of the slice: x: 2, y: 2, z: 4, core: 2. Of those that a mesh axis runs over, the one named last changes fastest.
Arguments:
- intensity: float32 [16, 131072], P('phase', ('groups', 'space')), parts along dimension 1, may hold values from -6 to 6
- image_grad: bfloat16 [3, 16, 131072], P(None, 'phase', ('groups', 'space')), parts along dimension 2, may hold values from -6 to 6
- owner: int32 [131072, 1], P(('groups', 'space')), parts along dimension 0, may hold values from 0 to 3; in each aligned block of 16384 rows (0 to 16383, 16384 to 32767, ...) at most 8192 rows name the same one
- coord_xy: int32 [2, 131072], P(None, ('groups', 'space')), parts along dimension 1, may hold values from 0 to 463
- coord_z: int32 [131072], P(('groups', 'space')), parts along dimension 0, may hold values from 0 to 127
Outputs:
- control_grad: float32 [6, 16, 32, 1024], P('groups', 'phase', 'space'), parts along dimension 0
There are 2 independent parts, one for each index of `groups`. A program takes and returns all parts, laid end to end along the dimension named above; each array names one. Nothing has to cross between parts.
Inputs may be any that keep to these rules, and one draw needn't show every extreme that they name: Of the samples of one device, at most 8192 name the same owner, and some device has exactly 8192 samples for some owner.
All inputs are finite; a program needn't handle non-finite values.
Results may differ from a plain program's by a relative error of at most 0.0041.
Values sent between devices are 32-bit elements; how exact they have to be, the bound alone decides.
No kernel may reach another device: no remote copies, remote signals or barrier semaphores. Data moves between devices by JAX's collectives and lax.ppermute only.
A program may use at most 64 MiB of HBM per device.

v0:
```python
import jax
import jax.numpy as jnp
from jax import lax
from jax.sharding import PartitionSpec as P

GX = 32
SPC = 16
GZ_DEV = 8


def shifted(block, axis, distance):
    devices = range(lax.axis_size(axis))
    route = [(i - distance, i) for i in devices if i - distance in devices]
    return lax.ppermute(block, axis, route)


def spline_values(offset):
    square = offset * offset
    cube = square * offset
    remain = 1.0 - offset
    return (
        remain * remain * remain / 6.0,
        (3.0 * cube - 6.0 * square + 4.0) / 6.0,
        (-3.0 * cube + 3.0 * square + 3.0 * offset + 1.0) / 6.0,
        cube / 6.0,
    )


def spread(position, extent):
    corner = jnp.floor(position)
    offset = position - corner
    values = spline_values(offset)
    distance = jnp.arange(extent, dtype=jnp.int32)[None, :] - corner.astype(jnp.int32)[:, None]
    weights = jnp.zeros((position.shape[0], extent), jnp.float32)
    for which, value in enumerate(values):
        weights = jnp.where(distance == which, value[:, None], weights)
    return weights


def block_grad(forces, positions):
    along_x = spread(positions[0], GX)
    along_y = spread(positions[1], GX)
    along_z = spread(positions[2], GZ_DEV + 3)
    plane = (along_x[:, :, None] * along_y[:, None, :]).reshape(-1, GX * GX).astype(jnp.bfloat16)
    lifted = (
        (forces[:, None, :] * along_z.T[None, :, :])
        .reshape(-1, forces.shape[1])
        .astype(jnp.bfloat16)
    )
    return jnp.dot(lifted, plane, preferred_element_type=jnp.float32)


def local(intensity, image_grad, owner, coord_xy, coord_z):
    ph_dev, s_dev = intensity.shape
    n_space = lax.axis_size("space")
    capacity = 2 * s_dev // n_space
    force_rows = 3 * ph_dev
    panels = lax.all_gather(intensity, "phase", axis=0, tiled=True)
    phase_mean = jnp.mean(panels, axis=0)
    centered_all = panels - phase_mean
    phase_var = jnp.mean(centered_all * centered_all, axis=0)
    deviation = 2.0 * (intensity - phase_mean) / jnp.sqrt(phase_var + 1.0)
    forces = (deviation[None] * image_grad.astype(jnp.float32)).reshape(force_rows, s_dev)
    positions = jnp.stack(
        [
            coord_xy[0].astype(jnp.float32) / SPC,
            coord_xy[1].astype(jnp.float32) / SPC,
            coord_z.astype(jnp.float32) / SPC,
        ],
        axis=0,
    )
    payload = jnp.concatenate([forces, positions], axis=0)
    target = owner[:, 0]
    matches = (target[:, None] == jnp.arange(n_space, dtype=jnp.int32)[None, :]).astype(jnp.int32)
    order_in = jnp.cumsum(matches, axis=0) - 1
    slot_index = jnp.sum(order_in * matches, axis=1)
    empty = jnp.concatenate(
        [
            jnp.zeros((n_space, force_rows, capacity), jnp.float32),
            -jnp.ones((n_space, 3, capacity), jnp.float32),
        ],
        axis=1,
    )
    buckets = empty.at[target, :, slot_index].set(payload.T)
    received = lax.all_to_all(buckets, "space", split_axis=0, concat_axis=0, tiled=True)
    start_grid = jnp.zeros((force_rows * (GZ_DEV + 3), GX * GX), jnp.float32)
    used_rows = jnp.sum((received[:, force_rows, :] >= 0.0).astype(jnp.int32), axis=1)
    step_rows = min(512, capacity)

    def add_bucket(bucket, running_grid):
        bucket_rows = received[bucket]

        def add_block(block_id, inner_grid):
            section = lax.dynamic_slice_in_dim(bucket_rows, block_id * step_rows, step_rows, 1)
            return inner_grid + block_grad(section[:force_rows], section[force_rows:])

        block_total = (used_rows[bucket] + step_rows - 1) // step_rows
        return lax.fori_loop(0, block_total, add_block, running_grid)

    local_grid = lax.fori_loop(0, n_space, add_bucket, start_grid)
    planes = local_grid.reshape(force_rows, GZ_DEV + 3, GX * GX)
    owned_planes = planes[:, :GZ_DEV]
    ghost_rows = planes[:, GZ_DEV:]
    incoming = shifted(ghost_rows, "space", 1)
    owned_planes = owned_planes.at[:, :3].add(incoming)
    return owned_planes.reshape(3, ph_dev, GZ_DEV, GX * GX)


def solution(mesh):
    return jax.shard_map(
        local,
        mesh=mesh,
        in_specs=(
            P("phase", ("groups", "space")),
            P(None, "phase", ("groups", "space")),
            P(("groups", "space"), None),
            P(None, ("groups", "space")),
            P(("groups", "space")),
        ),
        out_specs=P("groups", "phase", "space", None),
        check_vma=False,
    )
```

profile of v0, /device:TPU:8, one launch (start us, length us, event | category | flops | bytes accessed | tf_op | source)
XLA Modules:
  0.0 255.0 jit_solution(12700552280051949923)
XLA Ops:
  6.5 0.7 all-gather.3.cloned.1.call-update
  7.3 0.9 copy.18
  9.0 1.2 fusion.40
  10.2 1.0 compare_select_fusion
  11.1 1.1 convert_multiply_fusion.3
  12.3 0.9 multiply_reduce_fusion.1
  13.2 1.0 and_reduce_fusion
  14.2 0.8 convert_multiply_fusion.1
  15.0 11.7 %all-gather.3.cloned.1.call-done = f32[4,4,16384]{2,1,0:T(4,128)} async-done(((f32[1,4,16384]{2,1,0:T(4,128)}), f32[4,4,16384]{2,1,0:T(4,128)}) %all-gather.3.cloned.1.call-update) | async-done | bytes 1048592 | tf_op jit(solution)/shard_map/all_gather | solution.py:58
  26.8 1.5 reduce_sum.40
  28.3 1.6 reshape.506
  30.9 4.7 %copy.20 = f32[16384,15]{1,0:T(8,128)} copy(f32[16384,15]{0,1:T(8,128)S(1)} %maximum_bitcast_fusion) | data formatting | bytes 1966080 | tf_op jit(solution)/shard_map/transpose | solution.py:84
  35.6 6.0 %broadcast.556 = f32[15,32768]{0,1:T(8,128)} broadcast(f32[15]{0:T(128)S(1)} %concatenate.13), dimensions={0} | broadcast | bytes 1966140
  41.6 52.1 %scatter_fusion = f32[15,32768]{0,1:T(8,128)} fusion(f32[15,32768]{0,1:T(8,128)} %broadcast.556, s32[16384]{0:T(1024)S(1)} %broadcast_select_fusion, f32[16384,15]{1,0:T(8,128)} %copy.20), kind=kCustom, calls=%fused_computation | custom fusion | bytes 3014656
  93.7 10.8 %copy.21 = f32[15,4,8192]{2,0,1:T(8,128)} copy(f32[15,4,8192]{0,2,1:T(8,128)} %bitcast.50) | data formatting | bytes 3932160
  104.4 5.1 %all-to-all-start = ((f32[4,15,8192]{2,1,0:T(8,128)}), f32[4,15,8192]{2,1,0:T(8,128)}, u32[]{:S(2)}, u32[]{:S(2)}) async-start(f32[4,15,8192]{2,1,0:T(8,128)} %bitcast.15), calls=%async_computation | async-start | bytes 4194304 | tf_op jit(solution)/shard_map/all_to_all | solution.py:85
  109.6 45.4 %all-to-all-done = f32[4,15,8192]{2,1,0:T(8,128)} async-done(((f32[4,15,8192]{2,1,0:T(8,128)}), f32[4,15,8192]{2,1,0:T(8,128)}, u32[]{:S(2)}, u32[]{:S(2)}) %all-to-all-start) | async-done | bytes 1966112 | tf_op jit(solution)/shard_map/all_to_all | solution.py:85
  155.0 1.6 fusion.42
  156.6 81.8 %while.54 = (s32[]{:T(128)}, f32[132,1024]{1,0:T(8,128)S(1)}, s32[4]{0:T(128)S(1)}, f32[4,15,8192]{2,1,0:T(8,128)}, s32[]{:T(128)}, /*index=5*/s32[]{:T(128)}, s...) while((s32[]{:T(128)}, f32[132,1024]{1,0:T(8,128)S(1)}, ...), condition=%wide.region_10.11_spmd, body=%wide.region_7.10_spmd.sunk | while | flops 140110352 | bytes 5163650 | solution.py:100
  156.6 0.6 dynamic_slice.35
  157.9 1.1 dynamic-slice_bitcast_fusion.2
  158.9 18.1 %while.55 = (s32[]{:T(128)}, f32[132,1024]{1,0:T(8,128)S(1)}, s32[]{:T(128)}, f32[15,8192]{1,0:T(8,128)S(1)}, s32[]{:T(128)}, /*index=5*/s32[]{:T(128)}, s32[]{}, s32[]{:T(128)}, s32[]{:T(128)}, s32[]{}, /*index=10*/s32[]{}) while((s32[]{:T(128)}, f32[132,1024]{1,0:T(8,128)S(1)}, s32[]{:T(128)}, f32[15,8192]{1,0:T(8,128)S(1)}, s32[]{:T(128)}, ...), condition=%wide.region_9.9_spmd, body=%wide.region_8.8_spmd.sunk | while | flops 140110336 | bytes 4180179 | solution.py:98
  159.6 0.5 convolution_add_fusion.2
  161.8 0.5 convolution_add_fusion.2
  163.0 0.5 convolution_add_fusion.2
  165.2 0.5 convolution_add_fusion.2
  166.4 0.5 convolution_add_fusion.2
  168.6 0.5 convolution_add_fusion.2
  169.7 0.5 convolution_add_fusion.2
  172.0 0.5 convolution_add_fusion.2
  173.1 0.5 convolution_add_fusion.2
  176.5 0.5 convolution_add_fusion.2
  177.1 0.6 dynamic_slice.35
  178.3 1.1 dynamic-slice_bitcast_fusion.2
  179.4 18.1 %while.55 = (s32[]{:T(128)}, f32[132,1024]{1,0:T(8,128)S(1)}, s32[]{:T(128)}, f32[15,8192]{1,0:T(8,128)S(1)}, s32[]{:T(128)}, /*index=5*/s32[]{:T(128)}, s32[]{}, s32[]{:T(128)}, s32[]{:T(128)}, s32[]{}, /*index=10*/s32[]{}) while((s32[]{:T(128)}, f32[132,1024]{1,0:T(8,128)S(1)}, s32[]{:T(128)}, f32[15,8192]{1,0:T(8,128)S(1)}, s32[]{:T(128)}, ...), condition=%wide.region_9.9_spmd, body=%wide.region_8.8_spmd.sunk | while | flops 140110336 | bytes 4180179 | solution.py:98
  180.0 0.5 convolution_add_fusion.2
  183.4 0.5 convolution_add_fusion.2
  185.7 0.5 convolution_add_fusion.2
  186.8 0.5 convolution_add_fusion.2
  190.2 0.5 convolution_add_fusion.2
  193.6 0.5 convolution_add_fusion.2
  197.0 0.5 convolution_add_fusion.2
  197.5 0.6 dynamic_slice.35
  198.8 1.1 dynamic-slice_bitcast_fusion.2
  199.8 18.1 %while.55 = (s32[]{:T(128)}, f32[132,1024]{1,0:T(8,128)S(1)}, s32[]{:T(128)}, f32[15,8192]{1,0:T(8,128)S(1)}, s32[]{:T(128)}, /*index=5*/s32[]{:T(128)}, s32[]{}, s32[]{:T(128)}, s32[]{:T(128)}, s32[]{}, /*index=10*/s32[]{}) while((s32[]{:T(128)}, f32[132,1024]{1,0:T(8,128)S(1)}, s32[]{:T(128)}, f32[15,8192]{1,0:T(8,128)S(1)}, s32[]{:T(128)}, ...), condition=%wide.region_9.9_spmd, body=%wide.region_8.8_spmd.sunk | while | flops 140110336 | bytes 4180179 | solution.py:98
  200.5 0.5 convolution_add_fusion.2
  203.9 0.5 convolution_add_fusion.2
  207.3 0.5 convolution_add_fusion.2
  210.7 0.5 convolution_add_fusion.2
  214.1 0.5 convolution_add_fusion.2
  217.4 0.5 convolution_add_fusion.2
  218.0 0.6 dynamic_slice.35
  219.2 1.1 dynamic-slice_bitcast_fusion.2
  220.3 18.1 %while.55 = (s32[]{:T(128)}, f32[132,1024]{1,0:T(8,128)S(1)}, s32[]{:T(128)}, f32[15,8192]{1,0:T(8,128)S(1)}, s32[]{:T(128)}, /*index=5*/s32[]{:T(128)}, s32[]{}, s32[]{:T(128)}, s32[]{:T(128)}, s32[]{}, /*index=10*/s32[]{}) while((s32[]{:T(128)}, f32[132,1024]{1,0:T(8,128)S(1)}, s32[]{:T(128)}, f32[15,8192]{1,0:T(8,128)S(1)}, s32[]{:T(128)}, ...), condition=%wide.region_9.9_spmd, body=%wide.region_8.8_spmd.sunk | while | flops 140110336 | bytes 4180179 | solution.py:98
  220.9 0.5 convolution_add_fusion.2
  224.3 0.5 convolution_add_fusion.2
  227.7 0.5 convolution_add_fusion.2
  231.1 0.5 convolution_add_fusion.2
  234.5 0.5 convolution_add_fusion.2
  237.9 0.5 convolution_add_fusion.2
  238.6 1.9 collective-permute-start
  240.5 5.9 %collective-permute-done = f32[12,3,1024]{2,1,0:T(4,128)S(1)} collective-permute-done((f32[12,3,1024]{2,1,0:T(4,128)S(1)}, f32[12,3,1024]{2,1,0:T(4,128)S(1)}, u32[]{:S(2)}, u32[]{:S(2)}) %collective-permute-start) | collective-permute-done | bytes 147488 | tf_op jit(solution)/shard_map/ppermute | solution.py:14
  246.5 0.9 scatter-add.4
  247.4 0.7 copy-done.1
  (703 shorter events, 54.5 us)
Async XLA Ops:
  6.5 23.6 %copy-start = (f32[4,16384]{1,0:T(4,128)S(1)}, f32[4,16384]{1,0:T(4,128)}, u32[]{:S(2)}) copy-start(f32[4,16384]{1,0:T(4,128)} %param.11) | copy-start | bytes 786436
  6.5 23.7 %copy-start.2 = (bf16[3,4,16384]{2,1,0:T(4,128)(2,1)S(1)}, bf16[3,4,16384]{2,1,0:T(4,128)(2,1)}, u32[]{:S(2)}) copy-start(bf16[3,4,16384]{2,1,0:T(4,128)(2,1)} %param.12) | copy-start | bytes 1179652
  6.5 20.2 %all-gather.3.cloned.1.call-start = ((), (), s32[]{:S(2)}) async-start(), calls=%async_computation.1 | async-start | bytes 1310720 | tf_op jit(solution)/shard_map/all_gather | solution.py:58
  104.4 50.5 %all-to-all-start = ((f32[4,15,8192]{2,1,0:T(8,128)}), f32[4,15,8192]{2,1,0:T(8,128)}, u32[]{:S(2)}, u32[]{:S(2)}) async-start(f32[4,15,8192]{2,1,0:T(8,128)} %bitcast.15), calls=%async_computation | async-start | bytes 4194304 | tf_op jit(solution)/shard_map/all_to_all | solution.py:85
  238.6 7.9 %collective-permute-start = (f32[12,3,1024]{2,1,0:T(4,128)S(1)}, f32[12,3,1024]{2,1,0:T(4,128)S(1)}, u32[]{:S(2)}, u32[]{:S(2)}) collective-permute-start(f32[12,3,1024]{2,1,0:T(4,128)S(1)} %slice.75), channel_id=1, source_target_pairs={{0,4},{4,8},{8,12},{1,5},{5,9},{9,13},{2,6},{6,10},{10,14},{3,7},{... | collective-permute-start | bytes 442376 | tf_op jit(solution)/shard_map/ppermute | solution.py:14
  247.4 0.7 copy-start.1
Sparse Core Ops, SparseCore 0:
  8.9 17.8 all-gather.2
where the time goes:
time: 256 us; the launch traced here: 255 us
  local copies, waits for them, and re-layouts  95.6 us (37%)
  waiting for transfers between devices  63.7 us (25%)
  other arithmetic  35 us (14%)
  matrix products  31.8 us (12%)
  between operations  13.6 us (5%)
  loops' own time  8.22 us (3%)
  starting transfers between devices  7.06 us (3%)
    unnamed x10, local copies, waits for them, and re-layouts  71.2 us
    all_to_all x1, waiting for transfers between devices, local(): lax.all_to_all(buckets, 'space', split_axis=0, concat_axis=0, tiled=True)  45.4 us
    dot_general x64, matrix products, block_grad(): return jnp.dot(lifted, plane, preferred_element_type=jnp.float32)  31.8 us
    convert_element_type x64, other arithmetic, block_grad(): (along_x[:, :, None] * along_y[:, None, :]).reshape(-1, GX * GX)  16.3 us
    all_gather x1, waiting for transfers between devices, local(): panels = lax.all_gather(intensity, 'phase', axis=0, tiled=True)  11.7 us
    ppermute x1, waiting for transfers between devices, shifted(): return lax.ppermute(block, axis, route)  5.9 us
    slice x64, local copies, waits for them, and re-layouts, block_grad(): along_x = spread(positions[0], GX)  5.76 us
    another operation x4, loops' own time, add_bucket(): return lax.fori_loop(0, block_total, add_block, running_grid)  5.55 us
  transfers between devices with their start and end apart: 3, of which 3 were waited for; matrix products, arithmetic and copies ran while one was open for 3% of the time, Pallas kernels for 0%

commit v1 on v0

v1 whole, which is shorter than its diff:
```python
import functools

import jax
import jax.numpy as jnp
from jax import lax
from jax.experimental import pallas as pl
from jax.experimental.pallas import tpu as pltpu
from jax.sharding import PartitionSpec as P

GX = 32
SPC = 16
GZ_DEV = 8
PIECES = 1
K_BLOCK = 1024
SUB = 256


def stats_kernel(intensity_ref, out_ref):
    values = intensity_ref[...]
    mean = jnp.mean(values, axis=0, keepdims=True)
    centered = values - mean
    out_ref[0:1] = mean
    out_ref[1:2] = jnp.sum(centered * centered, axis=0, keepdims=True)


def spline_weights(position, extent, first):
    shape = (extent, position.shape[1])
    index = lax.broadcasted_iota(jnp.int32, shape, 0) + first
    away = jnp.abs(index.astype(jnp.float32) - (position + 1.0))
    wide = jnp.maximum(2.0 - away, 0.0)
    near = jnp.maximum(1.0 - away, 0.0)
    return (wide * wide * wide - 4.0 * (near * near * near)) * (1.0 / 6.0)


def grid_kernel(
    intensity_ref, grad_ref, stats_ref, owner_ref, xy_ref, z_ref, out_ref,
    lifted_a, lifted_b, plane_a, plane_b,
    *, planes, phases, first_x, width_x,
):
    ph_dev, samples = intensity_ref.shape
    blocks = samples // K_BLOCK

    def build(block, lifted, plane):
        for sub in range(K_BLOCK // SUB):
            here = pl.ds(pl.multiple_of(block * K_BLOCK + sub * SUB, SUB), SUB)
            cols = slice(sub * SUB, (sub + 1) * SUB)
            mean = stats_ref[0:1, here]
            var = stats_ref[1:2, here] * (1.0 / phases)
            scale = 2.0 / jnp.sqrt(var + 1.0)
            deviation = (intensity_ref[:, here] - mean) * scale
            pos_x = xy_ref[0:1, here].astype(jnp.float32) * (1.0 / SPC)
            pos_y = xy_ref[1:2, here].astype(jnp.float32) * (1.0 / SPC)
            pos_z = z_ref[0:1, here].astype(jnp.float32) * (1.0 / SPC)
            pos_z = pos_z + (owner_ref[0:1, here] * GZ_DEV).astype(jnp.float32)
            along_z = spline_weights(pos_z, planes, 0)
            for c in range(3):
                force = deviation * grad_ref[c, :, here].astype(jnp.float32)
                for p in range(ph_dev):
                    row = (c * ph_dev + p) * planes
                    lifted[row:row + planes, cols] = (force[p:p + 1] * along_z).astype(jnp.bfloat16)
            along_y = spline_weights(pos_y, GX, 0)
            along_x = spline_weights(pos_x, width_x, first_x)
            for x in range(width_x):
                plane[x * GX:(x + 1) * GX, cols] = (along_x[x:x + 1] * along_y).astype(jnp.bfloat16)

    def multiply(lifted, plane):
        return lax.dot_general(
            lifted[...], plane[...], (((1,), (1,)), ((), ())),
            preferred_element_type=jnp.float32)

    out_ref[...] = jnp.zeros(out_ref.shape, jnp.float32)
    build(0, lifted_a, plane_a)

    def pair(i, carry):
        build(2 * i + 1, lifted_b, plane_b)
        out_ref[...] += multiply(lifted_a, plane_a)
        build(jnp.minimum(2 * i + 2, blocks - 1), lifted_a, plane_a)
        out_ref[...] += multiply(lifted_b, plane_b)
        return carry

    lax.fori_loop(0, blocks // 2, pair, 0)


def partial_grid(intensity, image_grad, stats, owner, coord_xy, coord_z, planes, phases, piece, pieces):
    ph_dev = intensity.shape[0]
    width_x = GX // pieces
    rows = 3 * ph_dev * planes
    return pl.pallas_call(
        functools.partial(grid_kernel, planes=planes, phases=phases,
                          first_x=piece * width_x, width_x=width_x),
        out_shape=jax.ShapeDtypeStruct((rows, width_x * GX), jnp.float32),
        scratch_shapes=[
            pltpu.VMEM((rows, K_BLOCK), jnp.bfloat16),
            pltpu.VMEM((rows, K_BLOCK), jnp.bfloat16),
            pltpu.VMEM((width_x * GX, K_BLOCK), jnp.bfloat16),
            pltpu.VMEM((width_x * GX, K_BLOCK), jnp.bfloat16),
        ],
        compiler_params=pltpu.CompilerParams(vmem_limit_bytes=56 << 20),
    )(intensity, image_grad, stats, owner, coord_xy, coord_z).reshape(3 * ph_dev, planes, width_x * GX)


def phase_stats(intensity):
    ph_dev, samples = intensity.shape
    size = lax.axis_size("phase")
    stats = pl.pallas_call(
        stats_kernel, out_shape=jax.ShapeDtypeStruct((2, samples), jnp.float32))(intensity)
    count = float(ph_dev)
    step = 1
    while step < size:
        other = lax.ppermute(stats, "phase", [(i, i ^ step) for i in range(size)])
        gap = other[0] - stats[0]
        stats = jnp.stack([
            0.5 * (stats[0] + other[0]),
            stats[1] + other[1] + gap * gap * (0.5 * count)])
        count *= 2.0
        step *= 2
    return stats


def scatter_planes(partial):
    size = lax.axis_size("space")
    me = lax.axis_index("space")

    def own(target):
        return lax.dynamic_slice_in_dim(
            partial, jnp.clip(target, 0, size - 1) * GZ_DEV, GZ_DEV, 1)

    up = own(size - 1)
    down = own(0)
    for step in range(1, size):
        if step > 1:
            up = up + own(size + me - step)
            down = down + own(me + step - size)
        up = lax.ppermute(up, "space", [(i, i + 1) for i in range(min(step, size - 1))])
        down = lax.ppermute(down, "space", [(size - 1 - i, size - 2 - i) for i in range(min(step, size - 1))])
    return own(me) + up + down


def local(intensity, image_grad, owner, coord_xy, coord_z):
    ph_dev, samples = intensity.shape
    planes = lax.axis_size("space") * GZ_DEV
    phases = ph_dev * lax.axis_size("phase")
    stats = phase_stats(intensity)
    owner = owner.reshape(1, samples)
    coord_z = coord_z.reshape(1, samples)
    partial = partial_grid(intensity, image_grad, stats, owner, coord_xy, coord_z, planes, phases, 0, 1)
    mine = scatter_planes(partial)
    return mine.reshape(3, ph_dev, GZ_DEV, GX * GX)


def solution(mesh):
    return jax.shard_map(
        local,
        mesh=mesh,
        in_specs=(
            P("phase", ("groups", "space")),
            P(None, "phase", ("groups", "space")),
            P(("groups", "space"), None),
            P(None, ("groups", "space")),
            P(("groups", "space")),
        ),
        out_specs=P("groups", "phase", "space", None),
        check_vma=False,
    )
```

time: 256 us -> 78 us (0.30)
  the two profiles are of different devices: /device:TPU:8 before, /device:TPU:0 now
where the time goes in v1:
time: 78 us; the launch traced here: 77.7 us
  waiting for transfers between devices  27 us (35%)
  Pallas kernels  23.5 us (30%)
  starting transfers between devices  22.5 us (29%)
  other arithmetic  3.24 us (4%)
  local copies, waits for them, and re-layouts  1.29 us (2%)
    pallas_call x1, Pallas kernels, partial_grid(): pl.pallas_call(functools.partial(grid_kernel, planes=planes, phases=phase...  21.6 us
    ppermute x3, waiting for transfers between devices, scatter_planes(): lax.ppermute(up, 'space', [(i, i + 1) for i in range(min(step, size - 1))])  17.8 us
    ppermute x3, starting transfers between devices, scatter_planes(): lax.ppermute(up, 'space', [(i, i + 1) for i in range(min(step, size - 1))])  16.5 us
    ppermute x2, waiting for transfers between devices, phase_stats(): other = lax.ppermute(stats, 'phase', [(i, i ^ step) for i in range(size)])  5.01 us
    ppermute x3, waiting for transfers between devices, scatter_planes(): lax.ppermute(down, 'space', [(size - 1 - i, size - 2 - i) for i in range(...  4.14 us
    ppermute x2, starting transfers between devices, phase_stats(): other = lax.ppermute(stats, 'phase', [(i, i ^ step) for i in range(size)])  3.39 us
    ppermute x3, starting transfers between devices, scatter_planes(): lax.ppermute(down, 'space', [(size - 1 - i, size - 2 - i) for i in range(...  2.66 us
    pallas_call x1, Pallas kernels, phase_stats(): pl.pallas_call(stats_kernel, out_shape=jax.ShapeDtypeStruct((2, samples),...  1.96 us
  transfers between devices with their start and end apart: 8, of which 6 were waited for; matrix products, arithmetic and copies ran while one was open for 0% of the time, Pallas kernels for 0%

profile of v1, /device:TPU:0, one launch (start us, length us, event | category | flops | bytes accessed | tf_op | source)
XLA Modules:
  0.0 77.7 jit_solution(5426648196464448527)
XLA Ops:
  0.0 2.0 %shard_map.55 = f32[2,16384]{1,0:T(2,128)} custom-call(f32[4,16384]{1,0:T(4,128)} %intensity_ref.3), custom_call_target="tpu_custom_call" | custom-call | tf_op jit(solution)/shard_map/pallas_call | solution.py:105
  2.0 0.5 collective-permute-start
  2.4 1.2 %collective-permute-done = f32[2,16384]{1,0:T(2,128)S(1)} collective-permute-done((f32[2,16384]{1,0:T(2,128)}, f32[2,16384]{1,0:T(2,128)S(1)}, u32[]{:S(2)}, u32[]{:S(2)}) %collective-permute-start) | collective-permute-done | bytes 131104 | tf_op jit(solution)/shard_map/ppermute | solution.py:110
  3.6 1.2 %add_multiply_fusion.1 = (f32[1,16384]{1,0:T(1,128)S(1)}, f32[1,16384]{1,0:T(1,128)S(1)}) fusion(f32[2,16384]{1,0:T(2,128)S(1)} %collective-permute-done, f32[2,16384]{1,0:T(2,128)} %shard_map.55), kind=kLoop, calls=%fused_computation.12 | loop fusion | flops 114688 | bytes 393216 | tf_op jit(solution)/shard_map/mul | solution.py:113
  4.8 0.1 pad_maximum_fusion
  4.9 2.9 %collective-permute-start.1 = (f32[2,16384]{1,0:T(2,128)S(1)}, f32[2,16384]{1,0:T(2,128)S(1)}, u32[]{:S(2)}, u32[]{:S(2)}) collective-permute-start(f32[2,16384]{1,0:T(2,128)S(1)} %pad_maximum_fusion), channel_id=1, source_target_pairs={{0,2},{1,3},{2,0},{3,1},{4,6},{5,7},{6,4},{7,5},{8,10},{9,11},{10,... | collective-permute-start | bytes 393224 | tf_op jit(solution)/shard_map/ppermute | solution.py:110
  7.8 3.8 %collective-permute-done.1 = f32[2,16384]{1,0:T(2,128)S(1)} collective-permute-done((f32[2,16384]{1,0:T(2,128)S(1)}, f32[2,16384]{1,0:T(2,128)S(1)}, u32[]{:S(2)}, u32[]{:S(2)}) %collective-permute-start.1) | collective-permute-done | bytes 131104 | tf_op jit(solution)/shard_map/ppermute | solution.py:110
  11.7 0.2 add_multiply_fusion
  11.8 0.8 %pad_maximum_fusion.1.stats_ref = f32[2,16384]{1,0:T(2,128)} fusion(f32[1,16384]{1,0:T(1,128)S(1)} %get-tuple-element.14, f32[1,16384]{1,0:T(1,128)S(1)} %get-tuple-element.13), kind=kLoop, calls=%fused_computation.6 | loop fusion | flops 32768 | bytes 262144 | tf_op jit(solution)/shard_map/stack | solution.py:112
  12.6 21.6 %shard_map.56 = f32[384,1024]{1,0:T(8,128)} custom-call(f32[4,16384]{1,0:T(4,128)} %intensity_ref.3, bf16[3,4,16384]{2,1,0:T(4,128)(2,1)} %grad_ref.1, f32[2,16384]{1,0:T(2,128)} %pad_maximum_fusion.1.stats_ref, s32[1,16384]{1,0:T(1,128)} %bitcast.8, s32[2,16384]{1,0:T(2,128)} %xy_ref.1, s32[1,16384]{1,0:T(1,128)} %bitcast.9), custom_call_target="tpu_custom_call" | custom-call | tf_op jit(solution)/shard_map/pallas_call | solution.py:88
  34.2 0.0 copy-start
  34.2 1.3 %fusion.2 = (f32[12,8,1024]{2,1,0:T(8,128)S(1)}, f32[12,8,1024]{2,1,0:T(8,128)S(1)}) fusion(f32[12,32,1024]{2,1,0:T(8,128)} %bitcast.4), kind=kLoop, calls=%fused_computation.13 | loop fusion | bytes 1572864 | tf_op jit(solution)/shard_map/dynamic_slice | solution.py:125
  35.5 3.8 %collective-permute-start.2 = (f32[12,8,1024]{2,1,0:T(8,128)S(1)}, f32[12,8,1024]{2,1,0:T(8,128)S(1)}, u32[]{:S(2)}, u32[]{:S(2)}) collective-permute-start(f32[12,8,1024]{2,1,0:T(8,128)S(1)} %get-tuple-element.9), channel_id=1, source_target_pairs={{0,4},{1,5},{2,6},{3,7},{16,20},{17,21},{18,22},{19,23}} | collective-permute-start | bytes 1179656 | tf_op jit(solution)/shard_map/ppermute | solution.py:134
  39.2 0.7 collective-permute-start.5
  39.9 7.1 %collective-permute-done.2 = f32[12,8,1024]{2,1,0:T(8,128)S(1)} collective-permute-done((f32[12,8,1024]{2,1,0:T(8,128)S(1)}, f32[12,8,1024]{2,1,0:T(8,128)S(1)}, u32[]{:S(2)}, u32[]{:S(2)}) %collective-permute-start.2) | collective-permute-done | bytes 393248 | tf_op jit(solution)/shard_map/ppermute | solution.py:134
  47.0 0.0 collective-permute-done.5
  47.0 0.0 copy-done
  47.0 0.1 dynamic-slice_add_fusion.3
  47.1 4.4 %collective-permute-start.3 = (f32[12,8,1024]{2,1,0:T(8,128)S(1)}, f32[12,8,1024]{2,1,0:T(8,128)S(1)}, u32[]{:S(2)}, u32[]{:S(2)}) collective-permute-start(f32[12,8,1024]{2,1,0:T(8,128)S(1)} %get-tuple-element.7), channel_id=1, source_target_pairs={{0,4},{4,8},{1,5},{5,9},{2,6},{6,10},{3,7},{7,11},{16,20},{20,24},... | collective-permute-start | bytes 1179656 | tf_op jit(solution)/shard_map/ppermute | solution.py:134
  51.6 0.7 collective-permute-start.6
  52.3 6.2 %collective-permute-done.3 = f32[12,8,1024]{2,1,0:T(8,128)S(1)} collective-permute-done((f32[12,8,1024]{2,1,0:T(8,128)S(1)}, f32[12,8,1024]{2,1,0:T(8,128)S(1)}, u32[]{:S(2)}, u32[]{:S(2)}) %collective-permute-start.3) | collective-permute-done | bytes 393248 | tf_op jit(solution)/shard_map/ppermute | solution.py:134
  58.5 0.0 collective-permute-done.6
  58.5 0.1 dynamic-slice_add_fusion.2
  58.6 8.3 %collective-permute-start.4 = (f32[12,8,1024]{2,1,0:T(8,128)S(1)}, f32[12,8,1024]{2,1,0:T(8,128)S(1)}, u32[]{:S(2)}, u32[]{:S(2)}) collective-permute-start(f32[12,8,1024]{2,1,0:T(8,128)S(1)} %get-tuple-element.5), channel_id=1, source_target_pairs={{0,4},{4,8},{8,12},{1,5},{5,9},{9,13},{2,6},{6,10},{10,14},{3,7},{... | collective-permute-start | bytes 1179656 | tf_op jit(solution)/shard_map/ppermute | solution.py:134
  66.9 1.3 %collective-permute-start.7 = (f32[12,8,1024]{2,1,0:T(8,128)S(1)}, f32[12,8,1024]{2,1,0:T(8,128)S(1)}, u32[]{:S(2)}, u32[]{:S(2)}) collective-permute-start(f32[12,8,1024]{2,1,0:T(8,128)S(1)} %get-tuple-element.6), channel_id=1, source_target_pairs={{12,8},{8,4},{4,0},{13,9},{9,5},{5,1},{14,10},{10,6},{6,2},{15,11}... | collective-permute-start | bytes 1179656 | tf_op jit(solution)/shard_map/ppermute | solution.py:135
  68.2 4.5 %collective-permute-done.4 = f32[12,8,1024]{2,1,0:T(8,128)S(1)} collective-permute-done((f32[12,8,1024]{2,1,0:T(8,128)S(1)}, f32[12,8,1024]{2,1,0:T(8,128)S(1)}, u32[]{:S(2)}, u32[]{:S(2)}) %collective-permute-start.4) | collective-permute-done | bytes 393248 | tf_op jit(solution)/shard_map/ppermute | solution.py:134
  72.7 4.1 %collective-permute-done.7 = f32[12,8,1024]{2,1,0:T(8,128)S(1)} collective-permute-done((f32[12,8,1024]{2,1,0:T(8,128)S(1)}, f32[12,8,1024]{2,1,0:T(8,128)S(1)}, u32[]{:S(2)}, u32[]{:S(2)}) %collective-permute-start.7) | collective-permute-done | bytes 393248 | tf_op jit(solution)/shard_map/ppermute | solution.py:135
  76.9 0.8 %add_add_fusion = f32[12,8,1024]{2,1,0:T(8,128)} fusion(f32[12,8,1024]{2,1,0:T(8,128)S(1)} %collective-permute-done.7, f32[12,8,1024]{2,1,0:T(8,128)S(1)} %collective-permute-done.4, f32[12,32,1024]{2,1,0:T(8,128)S(1)} %bitcast.7, s32[]{:T(128)S(6)} %select_n.17), kind=kLoop, calls=%fused_computation.2 | loop fusion | flops 196608 | bytes 1572868 | tf_op jit(solution)/shard_map/add | solution.py:136
Async XLA Ops:
  2.0 1.7 %collective-permute-start = (f32[2,16384]{1,0:T(2,128)}, f32[2,16384]{1,0:T(2,128)S(1)}, u32[]{:S(2)}, u32[]{:S(2)}) collective-permute-start(f32[2,16384]{1,0:T(2,128)} %shard_map.55), channel_id=1, source_target_pairs={{0,1},{1,0},{2,3},{3,2},{4,5},{5,4},{6,7},{7,6},{8,9},{9,8},{10,11... | collective-permute-start | bytes 393224 | tf_op jit(solution)/shard_map/ppermute | solution.py:110
  4.9 6.7 %collective-permute-start.1 = (f32[2,16384]{1,0:T(2,128)S(1)}, f32[2,16384]{1,0:T(2,128)S(1)}, u32[]{:S(2)}, u32[]{:S(2)}) collective-permute-start(f32[2,16384]{1,0:T(2,128)S(1)} %pad_maximum_fusion), channel_id=1, source_target_pairs={{0,2},{1,3},{2,0},{3,1},{4,6},{5,7},{6,4},{7,5},{8,10},{9,11},{10,... | collective-permute-start | bytes 393224 | tf_op jit(solution)/shard_map/ppermute | solution.py:110
  34.2 12.8 %copy-start = (f32[384,1024]{1,0:T(8,128)S(1)}, f32[384,1024]{1,0:T(8,128)}, u32[]{:S(2)}) copy-start(f32[384,1024]{1,0:T(8,128)} %shard_map.56) | copy-start | bytes 4718596
  35.5 11.6 %collective-permute-start.2 = (f32[12,8,1024]{2,1,0:T(8,128)S(1)}, f32[12,8,1024]{2,1,0:T(8,128)S(1)}, u32[]{:S(2)}, u32[]{:S(2)}) collective-permute-start(f32[12,8,1024]{2,1,0:T(8,128)S(1)} %get-tuple-element.9), channel_id=1, source_target_pairs={{0,4},{1,5},{2,6},{3,7},{16,20},{17,21},{18,22},{19,23}} | collective-permute-start | bytes 1179656 | tf_op jit(solution)/shard_map/ppermute | solution.py:134
  39.2 7.8 %collective-permute-start.5 = (f32[12,8,1024]{2,1,0:T(8,128)S(1)}, f32[12,8,1024]{2,1,0:T(8,128)S(1)}, u32[]{:S(2)}, u32[]{:S(2)}) collective-permute-start(f32[12,8,1024]{2,1,0:T(8,128)S(1)} %get-tuple-element.10), channel_id=1, source_target_pairs={{12,8},{13,9},{14,10},{15,11},{28,24},{29,25},{30,26},{31,27}} | collective-permute-start | bytes 1179656 | tf_op jit(solution)/shard_map/ppermute | solution.py:135
  47.1 11.4 %collective-permute-start.3 = (f32[12,8,1024]{2,1,0:T(8,128)S(1)}, f32[12,8,1024]{2,1,0:T(8,128)S(1)}, u32[]{:S(2)}, u32[]{:S(2)}) collective-permute-start(f32[12,8,1024]{2,1,0:T(8,128)S(1)} %get-tuple-element.7), channel_id=1, source_target_pairs={{0,4},{4,8},{1,5},{5,9},{2,6},{6,10},{3,7},{7,11},{16,20},{20,24},... | collective-permute-start | bytes 1179656 | tf_op jit(solution)/shard_map/ppermute | solution.py:134
  51.6 6.9 %collective-permute-start.6 = (f32[12,8,1024]{2,1,0:T(8,128)S(1)}, f32[12,8,1024]{2,1,0:T(8,128)S(1)}, u32[]{:S(2)}, u32[]{:S(2)}) collective-permute-start(f32[12,8,1024]{2,1,0:T(8,128)S(1)} %get-tuple-element.8), channel_id=1, source_target_pairs={{12,8},{8,4},{13,9},{9,5},{14,10},{10,6},{15,11},{11,7},{28,24},{2... | collective-permute-start | bytes 1179656 | tf_op jit(solution)/shard_map/ppermute | solution.py:135
  58.6 14.1 %collective-permute-start.4 = (f32[12,8,1024]{2,1,0:T(8,128)S(1)}, f32[12,8,1024]{2,1,0:T(8,128)S(1)}, u32[]{:S(2)}, u32[]{:S(2)}) collective-permute-start(f32[12,8,1024]{2,1,0:T(8,128)S(1)} %get-tuple-element.5), channel_id=1, source_target_pairs={{0,4},{4,8},{8,12},{1,5},{5,9},{9,13},{2,6},{6,10},{10,14},{3,7},{... | collective-permute-start | bytes 1179656 | tf_op jit(solution)/shard_map/ppermute | solution.py:134
  66.9 9.9 %collective-permute-start.7 = (f32[12,8,1024]{2,1,0:T(8,128)S(1)}, f32[12,8,1024]{2,1,0:T(8,128)S(1)}, u32[]{:S(2)}, u32[]{:S(2)}) collective-permute-start(f32[12,8,1024]{2,1,0:T(8,128)S(1)} %get-tuple-element.6), channel_id=1, source_target_pairs={{12,8},{8,4},{4,0},{13,9},{9,5},{5,1},{14,10},{10,6},{6,2},{15,11}... | collective-permute-start | bytes 1179656 | tf_op jit(solution)/shard_map/ppermute | solution.py:135

commit v2 on v1

v2 whole, which is shorter than its diff:
```python
import functools

import jax
import jax.numpy as jnp
from jax import lax
from jax.experimental import pallas as pl
from jax.experimental.pallas import tpu as pltpu
from jax.sharding import PartitionSpec as P


GX = 32
SPC = 16
GZ_DEV = 8
K_BLOCK = 2048
SUB = 512
STEP = 512
SPLIT = (16, 16)
COST = pl.CostEstimate(flops=1 << 30, bytes_accessed=12 << 20, transcendentals=0)

IN_VMEM = pl.BlockSpec(memory_space=pltpu.VMEM)


def spline_weights(position, extent, first):
    shape = (extent, position.shape[1])
    index = lax.broadcasted_iota(jnp.int32, shape, 0) + first
    away = jnp.abs(index.astype(jnp.float32) - (position + 1.0))
    wide = jnp.maximum(2.0 - away, 0.0)
    near = jnp.maximum(1.0 - away, 0.0)
    return (wide * wide * wide - 4.0 * (near * near * near)) * (1.0 / 6.0)


def stats_kernel(intensity_ref, out_ref):
    values = intensity_ref[...]
    mean = jnp.mean(values, axis=0, keepdims=True)
    centered = values - mean
    out_ref[0:1] = mean
    out_ref[1:2] = jnp.sum(centered * centered, axis=0, keepdims=True)


def phase_stats(intensity):
    return pl.pallas_call(
        stats_kernel,
        out_shape=jax.ShapeDtypeStruct((2, intensity.shape[1]), jnp.float32),
        compiler_params=pltpu.CompilerParams(vmem_limit_bytes=4 << 20),
        cost_estimate=COST,
        name="phase_stats",
    )(intensity)


def weights_kernel(coord_ref, x_ref, y_ref):
    def step(i, carry):
        here = pl.ds(pl.multiple_of(i * STEP, STEP), STEP)
        for row, out_ref in enumerate((x_ref, y_ref)):
            position = coord_ref[row:row + 1, here].astype(jnp.float32) * (1.0 / SPC)
            out_ref[:, here] = spline_weights(position, GX, 0)
        return carry

    lax.fori_loop(0, coord_ref.shape[1] // STEP, step, 0)


def plane_weights(coord_xy):
    samples = coord_xy.shape[1]
    return pl.pallas_call(
        weights_kernel,
        out_shape=[jax.ShapeDtypeStruct((GX, samples), jnp.float32)] * 2,
        in_specs=[IN_VMEM],
        out_specs=[IN_VMEM, IN_VMEM],
        compiler_params=pltpu.CompilerParams(vmem_limit_bytes=4 << 20),
        cost_estimate=COST,
        name="plane_weights",
    )(coord_xy)


def forces_at(here, intensity_ref, grad_ref, stats_refs):
    ph_dev = intensity_ref.shape[0]
    means = [ref[0:1, here] for ref in stats_refs]
    mean = sum(means) * (1.0 / len(means))
    spread = sum(ref[1:2, here] for ref in stats_refs)
    spread = spread + sum((m - mean) * (m - mean) for m in means) * float(ph_dev)
    var = spread * (1.0 / (ph_dev * len(means)))
    deviation = (intensity_ref[:, here] - mean) * (2.0 / jnp.sqrt(var + 1.0))
    return [deviation * grad_ref[c, :, here].astype(jnp.float32) for c in range(3)]


def pair_kernel(*refs, n_stats, owners, first_x):
    *refs, lifted_a, lifted_b, plane_a, plane_b, total = refs
    if n_stats:
        intensity_ref, grad_ref, owner_ref, z_ref = refs[:4]
        stats_refs = refs[4:4 + n_stats]
        x_ref, y_ref, _, first_ref, second_ref, force_ref, height_ref = refs[4 + n_stats:]
    else:
        force_ref, height_ref, x_ref, y_ref, _, first_ref, second_ref = refs
    rows, samples = force_ref.shape
    half = rows * GZ_DEV
    blocks = samples // K_BLOCK
    firsts = [jnp.asarray(one * GZ_DEV, jnp.int32).astype(jnp.float32) for one in owners()]

    def prepare(here):
        ph_dev = rows // 3
        pos_z = z_ref[0:1, here].astype(jnp.float32) * (1.0 / SPC)
        height_ref[0:1, here] = pos_z + (owner_ref[0:1, here] * GZ_DEV).astype(jnp.float32)
        for c, force in enumerate(forces_at(here, intensity_ref, grad_ref, stats_refs)):
            force_ref[c * ph_dev:(c + 1) * ph_dev, here] = force

    def build(block, lifted, plane):
        for sub in range(K_BLOCK // SUB):
            here = pl.ds(pl.multiple_of(block * K_BLOCK + sub * SUB, SUB), SUB)
            cols = slice(sub * SUB, (sub + 1) * SUB)
            if n_stats:
                prepare(here)
            height = height_ref[0:1, here]
            for o, first_plane in enumerate(firsts):
                along_z = spline_weights(height - first_plane, GZ_DEV, 0)
                for r in range(0, rows, 2):
                    two = [force_ref[q:q + 1, here] * along_z for q in (r, r + 1)]
                    row = o * half + r * GZ_DEV
                    lifted[row:row + 2 * GZ_DEV, cols] = jnp.concatenate(two, axis=0).astype(jnp.bfloat16)
            along_y = y_ref[:, here]
            for x in range(plane.shape[0] // GX):
                along_x = x_ref[first_x + x:first_x + x + 1, here]
                plane[x * GX:(x + 1) * GX, cols] = (along_x * along_y).astype(jnp.bfloat16)

    def multiply(lifted, plane):
        return lax.dot_general(
            plane[...], lifted[...], (((1,), (1,)), ((), ())), preferred_element_type=jnp.float32)

    build(0, lifted_a, plane_a)
    total[...] = jnp.zeros(total.shape, jnp.float32)

    def pair(i, carry):
        build(2 * i + 1, lifted_b, plane_b)
        total[...] += multiply(lifted_a, plane_a)
        build(jnp.minimum(2 * i + 2, blocks - 1), lifted_a, plane_a)
        total[...] += multiply(lifted_b, plane_b)
        return carry

    lax.fori_loop(0, blocks // 2, pair, 0)
    both = total[...].T
    first_ref[...] = both[:half]
    second_ref[...] = both[half:]


def pair_grid(owners, args, first_x, width, after, stats=()):
    if stats:
        rows, samples = 3 * args[0].shape[0], args[0].shape[1]
    else:
        rows, samples = args[0].shape
    half = rows * GZ_DEV
    cells = width * GX
    out_shape = [jax.ShapeDtypeStruct((half, cells), jnp.float32)] * 2
    if stats:
        out_shape += [jax.ShapeDtypeStruct((rows, samples), jnp.float32),
                      jax.ShapeDtypeStruct((1, samples), jnp.float32)]
    outs = pl.pallas_call(
        functools.partial(pair_kernel, n_stats=len(stats), owners=owners, first_x=first_x),
        out_shape=out_shape,
        in_specs=[IN_VMEM for _ in args] + [pl.BlockSpec(memory_space=pl.ANY)],
        out_specs=[IN_VMEM for _ in out_shape],
        scratch_shapes=[
            pltpu.VMEM((2 * half, K_BLOCK), jnp.bfloat16),
            pltpu.VMEM((2 * half, K_BLOCK), jnp.bfloat16),
            pltpu.VMEM((cells, K_BLOCK), jnp.bfloat16),
            pltpu.VMEM((cells, K_BLOCK), jnp.bfloat16),
            pltpu.VMEM((cells, 2 * half), jnp.float32),
        ],
        compiler_params=pltpu.CompilerParams(vmem_limit_bytes=24 << 20),
        cost_estimate=COST,
        name="pair_grid",
    )(*args, after)
    return [o.reshape(rows, GZ_DEV, cells) for o in outs[:2]], outs[2:]


def from_other_phases(stats):
    size = lax.axis_size("phase")
    return [
        lax.ppermute(stats, "phase", [(i, (i + k) % size) for i in range(size)])
        for k in range(1, size)]


def chain(chunk_of):
    size = lax.axis_size("space")
    me = lax.axis_index("space")
    up = down = None
    for step in range(1, size):
        send_up, send_down = chunk_of(size + me - step), chunk_of(me + step - size)
        up = send_up if up is None else up + send_up
        down = send_down if down is None else down + send_down
        up = lax.ppermute(up, "space", [(i, i + 1) for i in range(step)])
        down = lax.ppermute(down, "space", [(size - 1 - i, size - 2 - i) for i in range(step)])
    total = chunk_of(me)
    return total if up is None else total + up + down


FIRST = [(0, 1), (1, 3), (3, 2), (2, 0)]
SIDE = [(0, 1), (1, 0), (2, 3), (3, 2)]
ACROSS = [(0, 3), (3, 0), (1, 2), (2, 1)]


def flipped(first, second):
    def owners():
        me = lax.axis_index("space")
        return me ^ first, me ^ second

    return owners


def inner_device():
    me = lax.axis_index("space")
    return (me == 1) | (me == 2)


def join_kernel(own_ref, got_ref, out_ref):
    out_ref[...] = own_ref[...] + jnp.where(inner_device(), got_ref[...], 0.0)


def finish_kernel(*refs):
    out_ref = refs[-1]
    start = 0
    for piece in range((len(refs) - 1) // 4):
        mine, side, first, across = refs[4 * piece:4 * piece + 4]
        cells = mine.shape[-1]
        out_ref[:, :, start:start + cells] = (
            mine[...] + side[...] + across[...] + jnp.where(inner_device(), 0.0, first[...]))
        start += cells


def in_vmem(kernel, shape, args, out_spec):
    return pl.pallas_call(
        kernel, out_shape=jax.ShapeDtypeStruct(shape, jnp.float32),
        in_specs=[IN_VMEM for _ in args], out_specs=out_spec,
        compiler_params=pltpu.CompilerParams(vmem_limit_bytes=8 << 20))(*args)


def four_owners(pair_of, pieces):
    firsts, acrosses, threes, args = [], [], [], []

    def relay(piece):
        joined = in_vmem(join_kernel, threes[piece].shape, (threes[piece], firsts[piece]), IN_VMEM)
        acrosses.append(lax.ppermute(joined, "space", ACROSS))
        return joined

    after = None
    for piece in range(pieces):
        two, three = pair_of(flipped(2, 3), piece, after)
        firsts.append(lax.ppermute(two, "space", FIRST))
        threes.append(three)
        after = two
    for piece in range(pieces):
        after = relay(piece)
        one, mine = pair_of(flipped(1, 0), piece, after)
        args += [mine, lax.ppermute(one, "space", SIDE), firsts[piece], acrosses[piece]]
    shape = mine.shape[:2] + (sum(a.shape[-1] for a in args[::4]),)
    return in_vmem(finish_kernel, shape, args, pl.BlockSpec())


def local(intensity, image_grad, owner, coord_xy, coord_z):
    ph_dev, samples = intensity.shape
    size = lax.axis_size("space")
    stats = phase_stats(intensity)
    stats = [stats] + from_other_phases(stats)
    weights = plane_weights(coord_xy)
    raw = [intensity, image_grad, owner.reshape(1, samples), coord_z.reshape(1, samples)]
    prepared = []

    def pair_of(owners, piece, after=None):
        first_x, width = sum(SPLIT[:piece]), SPLIT[piece]
        after = stats[0] if after is None else after
        if prepared:
            return pair_grid(owners, [*prepared, *weights], first_x, width, after)[0]
        outs, kept = pair_grid(owners, [*raw, *stats, *weights], first_x, width, after, stats=stats)
        prepared.extend(kept)
        return outs

    if size == 4:
        grid = four_owners(pair_of, len(SPLIT))
    else:
        columns = []
        for piece in range(len(SPLIT)):
            chunks = []
            for start in range(0, size, 2):
                chunks += pair_of(lambda start=start: (start, min(start + 1, size - 1)), piece)
            table = jnp.stack(chunks)
            columns.append(chain(lambda j: lax.dynamic_index_in_dim(
                table, jnp.clip(j, 0, size - 1), 0, keepdims=False)))
        grid = jnp.concatenate(columns, axis=-1)
    return grid.reshape(3, ph_dev, GZ_DEV, GX * GX)


def solution(mesh):
    return jax.shard_map(
        local,
        mesh=mesh,
        in_specs=(
            P("phase", ("groups", "space")),
            P(None, "phase", ("groups", "space")),
            P(("groups", "space"), None),
            P(None, ("groups", "space")),
            P(("groups", "space")),
        ),
        out_specs=P("groups", "phase", "space", None),
        check_vma=False,
    )
```

time: 78 us -> 54.2 us (0.69)
  starting transfers between devices: 22.5 us -> 10.4 us
  waiting for transfers between devices: 27 us -> 15.2 us
  Pallas kernels: 23.5 us -> 27.4 us
  other arithmetic: 3.24 us -> 0 us
    ppermute x8 -> x9, starting transfers between devices: 22.5 us -> 10.4 us  [the longest x2 4.44 us: four_owners(): firsts.append(lax.ppermute(two, 'space', FIRST))]
    ppermute x8 -> x9, waiting for transfers between devices: 27 us -> 15.2 us  [the longest x2 7.27 us: four_owners(): lax.ppermute(one, 'space', SIDE)]
    pallas_call x2 -> x9, Pallas kernels: 23.5 us -> 27.4 us  [the longest x4 24 us: pair_grid(): pl.pallas_call(functools.partial(pair_kernel, n_stats=len(stats), owners=...]
    mul x2 -> x0, other arithmetic: 1.34 us -> none  [phase_stats(): 0.5 * (stats[0] + other[0])]
    dynamic_slice x1 -> x0, local copies, waits for them, and re-layouts: 1.29 us -> none  [own(): lax.dynamic_slice_in_dim(partial, jnp.clip(target, 0, size - 1) * GZ_DEV,...]
    add x3 -> x0, other arithmetic: 1 us -> none  [the longest x1 0.81 us: scatter_planes(): return own(me) + up + down]
    unnamed x2 -> x12, local copies, waits for them, and re-layouts: 0.01 us -> 0.98 us
    another operation x2 -> x0, other arithmetic: 0.9 us -> none  [phase_stats(): jnp.stack([0.5 * (stats[0] + other[0]), stats[1] + other[1] + gap * gap *...]
  transfers between devices with their start and end apart: 8 -> 9, of which waited for: 6 -> 4; matrix products, arithmetic and copies ran while one was open for 0% -> 0% of each run, Pallas kernels for 0% -> 37%
where the time goes in v2:
time: 54.2 us; the launch traced here: 54 us
  Pallas kernels  27.4 us (51%)
  waiting for transfers between devices  15.2 us (28%)
  starting transfers between devices  10.4 us (19%)
  local copies, waits for them, and re-layouts  0.98 us (2%)
    pallas_call x4, Pallas kernels, pair_grid(): pl.pallas_call(functools.partial(pair_kernel, n_stats=len(stats), owners=...  24 us
    ppermute x2, waiting for transfers between devices, four_owners(): lax.ppermute(one, 'space', SIDE)  7.27 us
    ppermute x3, waiting for transfers between devices, from_other_phases(): lax.ppermute(stats, 'phase', [(i, (i + k) % size) for i in range(size)])  4.59 us
    ppermute x2, starting transfers between devices, four_owners(): firsts.append(lax.ppermute(two, 'space', FIRST))  4.44 us
    ppermute x2, waiting for transfers between devices, four_owners(): firsts.append(lax.ppermute(two, 'space', FIRST))  3.38 us
    ppermute x3, starting transfers between devices, from_other_phases(): lax.ppermute(stats, 'phase', [(i, (i + k) % size) for i in range(size)])  3.25 us
    pallas_call x1, Pallas kernels, plane_weights(): pl.pallas_call(weights_kernel, out_shape=[jax.ShapeDtypeStruct((GX, sampl...  2.16 us
    ppermute x2, starting transfers between devices, relay(): acrosses.append(lax.ppermute(joined, 'space', ACROSS))  2.05 us
  transfers between devices with their start and end apart: 9, of which 4 were waited for; matrix products, arithmetic and copies ran while one was open for 0% of the time, Pallas kernels for 37%

profile of v2, /device:TPU:0, one launch (start us, length us, event | category | flops | bytes accessed | tf_op | source)
XLA Modules:
  0.0 54.0 jit_solution(7325928897716921547)
XLA Ops:
  0.0 0.0 copy-start.1
  0.0 0.9 %copy-done.1 = f32[4,16384]{1,0:T(4,128)S(1)} copy-done((f32[4,16384]{1,0:T(4,128)S(1)}, f32[4,16384]{1,0:T(4,128)}, u32[]{:S(2)}) %copy-start.1) | copy-done | bytes 262168
  1.0 0.0 copy-start.5
  1.0 0.4 phase_stats.1.refs_4_.refs_10_
  1.3 0.0 copy-start
  1.3 0.0 copy-start.2
  1.3 0.0 copy-start.3
  1.3 0.0 copy-start.4
  1.4 2.5 %collective-permute-start.2 = (f32[2,16384]{1,0:T(2,128)S(1)}, f32[2,16384]{1,0:T(2,128)S(1)}, u32[]{:S(2)}, u32[]{:S(2)}) collective-permute-start(f32[2,16384]{1,0:T(2,128)S(1)} %phase_stats.1.refs_4_.refs_10_), channel_id=1, source_target_pairs={{0,3},{1,0},{2,1},{3,2},{4,7},{5,4},{6,5},{7,6},{8,11},{9,8},{10,9... | collective-permute-start | bytes 393224 | tf_op jit(solution)/shard_map/ppermute | solution.py:176
  3.8 0.6 %collective-permute-start.1 = (f32[2,16384]{1,0:T(2,128)S(1)}, f32[2,16384]{1,0:T(2,128)S(1)}, u32[]{:S(2)}, u32[]{:S(2)}) collective-permute-start(f32[2,16384]{1,0:T(2,128)S(1)} %phase_stats.1.refs_4_.refs_10_), channel_id=1, source_target_pairs={{0,2},{1,3},{2,0},{3,1},{4,6},{5,7},{6,4},{7,5},{8,10},{9,11},{10,... | collective-permute-start | bytes 393224 | tf_op jit(solution)/shard_map/ppermute | solution.py:176
  4.5 0.2 collective-permute-start
  4.6 0.0 copy-done.5
  4.6 2.2 %plane_weights.1 = (f32[32,16384]{1,0:T(8,128)S(1)}, f32[32,16384]{1,0:T(8,128)S(1)}) custom-call(s32[2,16384]{1,0:T(2,128)S(1)} %copy-done.5), custom_call_target="tpu_custom_call" | custom-call | flops 1073741824 | bytes 12582912 | tf_op jit(solution)/shard_map/plane_weights/pallas_call | solution.py:63
  6.8 0.8 %collective-permute-done.2.refs_7_ = f32[2,16384]{1,0:T(2,128)S(1)} collective-permute-done((f32[2,16384]{1,0:T(2,128)S(1)}, f32[2,16384]{1,0:T(2,128)S(1)}, u32[]{:S(2)}, u32[]{:S(2)}) %collective-permute-start.2) | collective-permute-done | bytes 131104 | tf_op jit(solution)/shard_map/ppermute | solution.py:176
  7.6 3.8 %collective-permute-done.1.refs_6_ = f32[2,16384]{1,0:T(2,128)S(1)} collective-permute-done((f32[2,16384]{1,0:T(2,128)S(1)}, f32[2,16384]{1,0:T(2,128)S(1)}, u32[]{:S(2)}, u32[]{:S(2)}) %collective-permute-start.1) | collective-permute-done | bytes 131104 | tf_op jit(solution)/shard_map/ppermute | solution.py:176
  11.4 0.0 collective-permute-done.refs_5_
  11.4 0.0 copy-done
  11.4 0.0 copy-done.2
  11.4 0.0 copy-done.3
  11.4 0.0 copy-done.4
  11.4 6.4 %pair_grid.4 = (f32[96,512]{1,0:T(8,128)S(1)}, f32[96,512]{1,0:T(8,128)S(1)}, f32[12,16384]{1,0:T(8,128)S(1)}, f32[1,16384]{1,0:T(1,128)S(1)}) custom-call(f32[4,16384]{1,0:T(4,128)S(1)} %copy-done.2, bf16[3,4,16384]{2,1,0:T(4,128)(2,1)S(1)} %copy-done, s32[1,16384]{1,0:T(1,128)S(1)} %bitcast.17, s32[1,16384]{1,0:T(1,128)S(1)} %bitcast.18, ...), custom_call_target="tpu_custom_call" | custom-call | flops 1073741824 | bytes 12582912 | tf_op jit(solution)/shard_map/pair_grid/pallas_call | solution.py:154
  17.8 1.8 %collective-permute-start.3 = (f32[12,8,512]{2,1,0:T(8,128)S(1)}, f32[12,8,512]{2,1,0:T(8,128)S(1)}, u32[]{:S(2)}, u32[]{:S(2)}) collective-permute-start(f32[12,8,512]{2,1,0:T(8,128)S(1)} %bitcast.11), channel_id=1, source_target_pairs={{0,4},{4,12},{12,8},{8,0},{1,5},{5,13},{13,9},{9,1},{2,6},{6,14},{... | collective-permute-start | bytes 589832 | tf_op jit(solution)/shard_map/ppermute | solution.py:245
  19.6 5.9 %pair_grid.6 = (f32[96,512]{1,0:T(8,128)S(1)}, f32[96,512]{1,0:T(8,128)S(1)}) custom-call(f32[12,16384]{1,0:T(8,128)S(1)} %get-tuple-element.19.refs_0_, f32[1,16384]{1,0:T(1,128)S(1)} %get-tuple-element.20.refs_1_, f32[32,16384]{1,0:T(8,128)S(1)} %get-tuple-element.17.refs_8_.refs_2_, f32[32,16384]{1,0:T(8,128)S(1)} %get-tuple-element.18.refs_9_.refs_3_, ...), custom_call_target="tpu_custom_call" | custom-call | flops 1073741824 | bytes 12582912 | tf_op jit(solution)/shard_map/pair_grid/pallas_call | solution.py:154
  25.5 2.6 %collective-permute-start.6 = (f32[12,8,512]{2,1,0:T(8,128)S(1)}, f32[12,8,512]{2,1,0:T(8,128)S(1)}, u32[]{:S(2)}, u32[]{:S(2)}) collective-permute-start(f32[12,8,512]{2,1,0:T(8,128)S(1)} %bitcast.20), channel_id=1, source_target_pairs={{0,4},{4,12},{12,8},{8,0},{1,5},{5,13},{13,9},{9,1},{2,6},{6,14},{... | collective-permute-start | bytes 589832 | tf_op jit(solution)/shard_map/ppermute | solution.py:245
  28.1 0.0 collective-permute-done.3.got_ref.refs_2_
  28.1 0.5 collective-permute-start.5
  28.6 5.8 %pair_grid.5 = (f32[96,512]{1,0:T(8,128)S(1)}, f32[96,512]{1,0:T(8,128)S(1)}) custom-call(f32[12,16384]{1,0:T(8,128)S(1)} %get-tuple-element.19.refs_0_, f32[1,16384]{1,0:T(1,128)S(1)} %get-tuple-element.20.refs_1_, f32[32,16384]{1,0:T(8,128)S(1)} %get-tuple-element.17.refs_8_.refs_2_, f32[32,16384]{1,0:T(8,128)S(1)} %get-tuple-element.18.refs_9_.refs_3_, ...), custom_call_target="tpu_custom_call" | custom-call | flops 1073741824 | bytes 12582912 | tf_op jit(solution)/shard_map/pair_grid/pallas_call | solution.py:154
  34.5 0.6 %collective-permute-start.4 = (f32[12,8,512]{2,1,0:T(8,128)S(1)}, f32[12,8,512]{2,1,0:T(8,128)S(1)}, u32[]{:S(2)}, u32[]{:S(2)}) collective-permute-start(f32[12,8,512]{2,1,0:T(8,128)S(1)} %bitcast.19), channel_id=1, source_target_pairs={{0,4},{4,0},{8,12},{12,8},{1,5},{5,1},{9,13},{13,9},{2,6},{6,2},{1... | collective-permute-start | bytes 589832 | tf_op jit(solution)/shard_map/ppermute | solution.py:251
  35.0 3.4 %collective-permute-done.6.got_ref.refs_6_ = f32[12,8,512]{2,1,0:T(8,128)S(1)} collective-permute-done((f32[12,8,512]{2,1,0:T(8,128)S(1)}, f32[12,8,512]{2,1,0:T(8,128)S(1)}, u32[]{:S(2)}, u32[]{:S(2)}) %collective-permute-start.6) | collective-permute-done | bytes 196640 | tf_op jit(solution)/shard_map/ppermute | solution.py:245
  38.4 5.9 %pair_grid.7 = (f32[96,512]{1,0:T(8,128)S(1)}, f32[96,512]{1,0:T(8,128)S(1)}) custom-call(f32[12,16384]{1,0:T(8,128)S(1)} %get-tuple-element.19.refs_0_, f32[1,16384]{1,0:T(1,128)S(1)} %get-tuple-element.20.refs_1_, f32[32,16384]{1,0:T(8,128)S(1)} %get-tuple-element.17.refs_8_.refs_2_, f32[32,16384]{1,0:T(8,128)S(1)} %get-tuple-element.18.refs_9_.refs_3_, ...), custom_call_target="tpu_custom_call" | custom-call | flops 1073741824 | bytes 12582912 | tf_op jit(solution)/shard_map/pair_grid/pallas_call | solution.py:154
  44.3 0.1 collective-permute-start.7
  44.4 1.6 %collective-permute-start.8 = (f32[12,8,512]{2,1,0:T(8,128)S(1)}, f32[12,8,512]{2,1,0:T(8,128)S(1)}, u32[]{:S(2)}, u32[]{:S(2)}) collective-permute-start(f32[12,8,512]{2,1,0:T(8,128)S(1)} %shard_map.56.refs_4_), channel_id=1, source_target_pairs={{0,12},{12,0},{4,8},{8,4},{1,13},{13,1},{5,9},{9,5},{2,14},{14,2},... | collective-permute-start | bytes 589832 | tf_op jit(solution)/shard_map/ppermute | solution.py:239
  45.9 0.0 collective-permute-done.5.refs_3_
  45.9 0.0 collective-permute-done.4.refs_1_
  45.9 7.3 %collective-permute-done.7.refs_5_ = f32[12,8,512]{2,1,0:T(8,128)S(1)} collective-permute-done((f32[12,8,512]{2,1,0:T(8,128)S(1)}, f32[12,8,512]{2,1,0:T(8,128)S(1)}, u32[]{:S(2)}, u32[]{:S(2)}) %collective-permute-start.7) | collective-permute-done | bytes 196640 | tf_op jit(solution)/shard_map/ppermute | solution.py:251
  53.2 0.0 collective-permute-done.8.refs_7_
  53.2 0.8 %shard_map.57 = f32[12,8,1024]{2,1,0:T(8,128)} custom-call(f32[12,8,512]{2,1,0:T(8,128)S(1)} %bitcast.15, f32[12,8,512]{2,1,0:T(8,128)S(1)} %collective-permute-done.4.refs_1_, f32[12,8,512]{2,1,0:T(8,128)S(1)} %collective-permute-done.3.got_ref.refs_2_, f32[12,8,512]{2,1,0:T(8,128)S(1)} %collective-permute-done.5.refs_3_, f32[12,8,512]{2,1,0:T(8,128)S(1)} %bitcast.16, ...), custom_call_target="tpu_custom_call" | custom-call | tf_op jit(solution)/shard_map/pallas_call | solution.py:228
  (2 shorter events, 0.1 us)
Async XLA Ops:
  0.0 0.9 %copy-start.1 = (f32[4,16384]{1,0:T(4,128)S(1)}, f32[4,16384]{1,0:T(4,128)}, u32[]{:S(2)}) copy-start(f32[4,16384]{1,0:T(4,128)} %refs_0_.1) | copy-start | bytes 786436
  1.0 3.7 %copy-start.5 = (s32[2,16384]{1,0:T(2,128)S(1)}, s32[2,16384]{1,0:T(2,128)}, u32[]{:S(2)}) copy-start(s32[2,16384]{1,0:T(2,128)} %coord_ref.1) | copy-start | bytes 393220
  1.3 10.1 %copy-start = (bf16[3,4,16384]{2,1,0:T(4,128)(2,1)S(1)}, bf16[3,4,16384]{2,1,0:T(4,128)(2,1)}, u32[]{:S(2)}) copy-start(bf16[3,4,16384]{2,1,0:T(4,128)(2,1)} %refs_1_.1) | copy-start | bytes 1179652
  1.3 10.0 %copy-start.2 = (f32[4,16384]{1,0:T(4,128)S(1)}, f32[4,16384]{1,0:T(4,128)}, u32[]{:S(2)}) copy-start(f32[4,16384]{1,0:T(4,128)} %refs_0_.1) | copy-start | bytes 786436
  1.3 10.0 %copy-start.3 = (s32[16384,1]{0,1:T(1,128)S(1)}, s32[16384,1]{0,1:T(1,128)}, u32[]{:S(2)}) copy-start(s32[16384,1]{0,1:T(1,128)} %param.7) | copy-start | bytes 196612
  1.3 10.0 %copy-start.4 = (s32[16384]{0:T(1024)S(1)}, s32[16384]{0:T(1024)}, u32[]{:S(2)}) copy-start(s32[16384]{0:T(1024)} %param.9) | copy-start | bytes 196612
  1.4 6.2 %collective-permute-start.2 = (f32[2,16384]{1,0:T(2,128)S(1)}, f32[2,16384]{1,0:T(2,128)S(1)}, u32[]{:S(2)}, u32[]{:S(2)}) collective-permute-start(f32[2,16384]{1,0:T(2,128)S(1)} %phase_stats.1.refs_4_.refs_10_), channel_id=1, source_target_pairs={{0,3},{1,0},{2,1},{3,2},{4,7},{5,4},{6,5},{7,6},{8,11},{9,8},{10,9... | collective-permute-start | bytes 393224 | tf_op jit(solution)/shard_map/ppermute | solution.py:176
  3.8 7.5 %collective-permute-start.1 = (f32[2,16384]{1,0:T(2,128)S(1)}, f32[2,16384]{1,0:T(2,128)S(1)}, u32[]{:S(2)}, u32[]{:S(2)}) collective-permute-start(f32[2,16384]{1,0:T(2,128)S(1)} %phase_stats.1.refs_4_.refs_10_), channel_id=1, source_target_pairs={{0,2},{1,3},{2,0},{3,1},{4,6},{5,7},{6,4},{7,5},{8,10},{9,11},{10,... | collective-permute-start | bytes 393224 | tf_op jit(solution)/shard_map/ppermute | solution.py:176
  4.5 6.9 %collective-permute-start = (f32[2,16384]{1,0:T(2,128)S(1)}, f32[2,16384]{1,0:T(2,128)S(1)}, u32[]{:S(2)}, u32[]{:S(2)}) collective-permute-start(f32[2,16384]{1,0:T(2,128)S(1)} %phase_stats.1.refs_4_.refs_10_), channel_id=1, source_target_pairs={{0,1},{1,2},{2,3},{3,0},{4,5},{5,6},{6,7},{7,4},{8,9},{9,10},{10,1... | collective-permute-start | bytes 393224 | tf_op jit(solution)/shard_map/ppermute | solution.py:176
  17.8 10.3 %collective-permute-start.3 = (f32[12,8,512]{2,1,0:T(8,128)S(1)}, f32[12,8,512]{2,1,0:T(8,128)S(1)}, u32[]{:S(2)}, u32[]{:S(2)}) collective-permute-start(f32[12,8,512]{2,1,0:T(8,128)S(1)} %bitcast.11), channel_id=1, source_target_pairs={{0,4},{4,12},{12,8},{8,0},{1,5},{5,13},{13,9},{9,1},{2,6},{6,14},{... | collective-permute-start | bytes 589832 | tf_op jit(solution)/shard_map/ppermute | solution.py:245
  25.5 12.9 %collective-permute-start.6 = (f32[12,8,512]{2,1,0:T(8,128)S(1)}, f32[12,8,512]{2,1,0:T(8,128)S(1)}, u32[]{:S(2)}, u32[]{:S(2)}) collective-permute-start(f32[12,8,512]{2,1,0:T(8,128)S(1)} %bitcast.20), channel_id=1, source_target_pairs={{0,4},{4,12},{12,8},{8,0},{1,5},{5,13},{13,9},{9,1},{2,6},{6,14},{... | collective-permute-start | bytes 589832 | tf_op jit(solution)/shard_map/ppermute | solution.py:245
  28.1 17.8 %collective-permute-start.5 = (f32[12,8,512]{2,1,0:T(8,128)S(1)}, f32[12,8,512]{2,1,0:T(8,128)S(1)}, u32[]{:S(2)}, u32[]{:S(2)}) collective-permute-start(f32[12,8,512]{2,1,0:T(8,128)S(1)} %shard_map.55.refs_4_), channel_id=1, source_target_pairs={{0,12},{12,0},{4,8},{8,4},{1,13},{13,1},{5,9},{9,5},{2,14},{14,2},... | collective-permute-start | bytes 589832 | tf_op jit(solution)/shard_map/ppermute | solution.py:239
  34.5 11.5 %collective-permute-start.4 = (f32[12,8,512]{2,1,0:T(8,128)S(1)}, f32[12,8,512]{2,1,0:T(8,128)S(1)}, u32[]{:S(2)}, u32[]{:S(2)}) collective-permute-start(f32[12,8,512]{2,1,0:T(8,128)S(1)} %bitcast.19), channel_id=1, source_target_pairs={{0,4},{4,0},{8,12},{12,8},{1,5},{5,1},{9,13},{13,9},{2,6},{6,2},{1... | collective-permute-start | bytes 589832 | tf_op jit(solution)/shard_map/ppermute | solution.py:251
  44.3 8.9 %collective-permute-start.7 = (f32[12,8,512]{2,1,0:T(8,128)S(1)}, f32[12,8,512]{2,1,0:T(8,128)S(1)}, u32[]{:S(2)}, u32[]{:S(2)}) collective-permute-start(f32[12,8,512]{2,1,0:T(8,128)S(1)} %bitcast.21), channel_id=1, source_target_pairs={{0,4},{4,0},{8,12},{12,8},{1,5},{5,1},{9,13},{13,9},{2,6},{6,2},{1... | collective-permute-start | bytes 589832 | tf_op jit(solution)/shard_map/ppermute | solution.py:251
  44.4 8.8 %collective-permute-start.8 = (f32[12,8,512]{2,1,0:T(8,128)S(1)}, f32[12,8,512]{2,1,0:T(8,128)S(1)}, u32[]{:S(2)}, u32[]{:S(2)}) collective-permute-start(f32[12,8,512]{2,1,0:T(8,128)S(1)} %shard_map.56.refs_4_), channel_id=1, source_target_pairs={{0,12},{12,0},{4,8},{8,4},{1,13},{13,1},{5,9},{9,5},{2,14},{14,2},... | collective-permute-start | bytes 589832 | tf_op jit(solution)/shard_map/ppermute | solution.py:239

commit v3 on v2

--- a/solution.py
+++ b/solution.py
@@ -11,10 +11,11 @@
 GX = 32
 SPC = 16
 GZ_DEV = 8
-K_BLOCK = 2048
+BLOCKS = (1024, 2048, 4096, 4608)
 SUB = 512
 STEP = 512
 SPLIT = (16, 16)
+NEAR_SPLIT = (20, 12)
 COST = pl.CostEstimate(flops=1 << 30, bytes_accessed=12 << 20, transcendentals=0)
 
 IN_VMEM = pl.BlockSpec(memory_space=pltpu.VMEM)
@@ -82,6 +83,17 @@
     return [deviation * grad_ref[c, :, here].astype(jnp.float32) for c in range(3)]
 
 
+def block_sizes(samples):
+    sizes, left = [], samples
+    for size in BLOCKS:
+        sizes.append(min(size, left))
+        left -= sizes[-1]
+    while left:
+        sizes.append(min(BLOCKS[-1], left))
+        left -= sizes[-1]
+    return [size for size in sizes if size]
+
+
 def pair_kernel(*refs, n_stats, owners, first_x):
     *refs, lifted_a, lifted_b, plane_a, plane_b, total = refs
     if n_stats:
@@ -92,7 +104,8 @@
         force_ref, height_ref, x_ref, y_ref, _, first_ref, second_ref = refs
     rows, samples = force_ref.shape
     half = rows * GZ_DEV
-    blocks = samples // K_BLOCK
+    sizes = block_sizes(samples)
+    begins = [sum(sizes[:i]) for i in range(len(sizes))]
     firsts = [jnp.asarray(one * GZ_DEV, jnp.int32).astype(jnp.float32) for one in owners()]
 
     def prepare(here):
@@ -103,8 +116,8 @@
             force_ref[c * ph_dev:(c + 1) * ph_dev, here] = force
 
     def build(block, lifted, plane):
-        for sub in range(K_BLOCK // SUB):
-            here = pl.ds(pl.multiple_of(block * K_BLOCK + sub * SUB, SUB), SUB)
+        for sub in range(sizes[block] // SUB):
+            here = pl.ds(begins[block] + sub * SUB, SUB)
             cols = slice(sub * SUB, (sub + 1) * SUB)
             if n_stats:
                 prepare(here)
@@ -120,21 +133,22 @@
                 along_x = x_ref[first_x + x:first_x + x + 1, here]
                 plane[x * GX:(x + 1) * GX, cols] = (along_x * along_y).astype(jnp.bfloat16)
 
-    def multiply(lifted, plane):
+    def multiply(block, lifted, plane):
+        size = sizes[block]
         return lax.dot_general(
-            plane[...], lifted[...], (((1,), (1,)), ((), ())), preferred_element_type=jnp.float32)
-
-    build(0, lifted_a, plane_a)
-    total[...] = jnp.zeros(total.shape, jnp.float32)
-
-    def pair(i, carry):
-        build(2 * i + 1, lifted_b, plane_b)
-        total[...] += multiply(lifted_a, plane_a)
-        build(jnp.minimum(2 * i + 2, blocks - 1), lifted_a, plane_a)
-        total[...] += multiply(lifted_b, plane_b)
-        return carry
-
-    lax.fori_loop(0, blocks // 2, pair, 0)
+            plane[:, :size], lifted[:, :size], (((1,), (1,)), ((), ())),
+            preferred_element_type=jnp.float32)
+
+    buffers = ((lifted_a, plane_a), (lifted_b, plane_b))
+    build(0, *buffers[0])
+    for block in range(len(sizes)):
+        if block + 1 < len(sizes):
+            build(block + 1, *buffers[(block + 1) % 2])
+        part = multiply(block, *buffers[block % 2])
+        if block:
+            total[...] += part
+        else:
+            total[...] = part
     both = total[...].T
     first_ref[...] = both[:half]
     second_ref[...] = both[half:]
@@ -147,6 +161,7 @@
         rows, samples = args[0].shape
     half = rows * GZ_DEV
     cells = width * GX
+    largest = max(block_sizes(samples))
     out_shape = [jax.ShapeDtypeStruct((half, cells), jnp.float32)] * 2
     if stats:
         out_shape += [jax.ShapeDtypeStruct((rows, samples), jnp.float32),
@@ -157,10 +172,10 @@
         in_specs=[IN_VMEM for _ in args] + [pl.BlockSpec(memory_space=pl.ANY)],
         out_specs=[IN_VMEM for _ in out_shape],
         scratch_shapes=[
-            pltpu.VMEM((2 * half, K_BLOCK), jnp.bfloat16),
-            pltpu.VMEM((2 * half, K_BLOCK), jnp.bfloat16),
-            pltpu.VMEM((cells, K_BLOCK), jnp.bfloat16),
-            pltpu.VMEM((cells, K_BLOCK), jnp.bfloat16),
+            pltpu.VMEM((2 * half, largest), jnp.bfloat16),
+            pltpu.VMEM((2 * half, largest), jnp.bfloat16),
+            pltpu.VMEM((cells, largest), jnp.bfloat16),
+            pltpu.VMEM((cells, largest), jnp.bfloat16),
             pltpu.VMEM((cells, 2 * half), jnp.float32),
         ],
         compiler_params=pltpu.CompilerParams(vmem_limit_bytes=24 << 20),
@@ -172,6 +187,10 @@
 
 def from_other_phases(stats):
     size = lax.axis_size("phase")
+    if size == 4:
+        chip = lax.ppermute(stats, "phase", [(i, i ^ 2) for i in range(size)])
+        core = lax.ppermute(stats, "phase", [(i, i ^ 1) for i in range(size)])
+        return [core, chip, lax.ppermute(chip, "phase", [(i, i ^ 1) for i in range(size)])]
     return [
         lax.ppermute(stats, "phase", [(i, (i + k) % size) for i in range(size)])
         for k in range(1, size)]
@@ -216,11 +235,17 @@
 def finish_kernel(*refs):
     out_ref = refs[-1]
     start = 0
-    for piece in range((len(refs) - 1) // 4):
-        mine, side, first, across = refs[4 * piece:4 * piece + 4]
+    for piece in range(len(NEAR_SPLIT)):
+        mine, side = refs[2 * piece:2 * piece + 2]
         cells = mine.shape[-1]
-        out_ref[:, :, start:start + cells] = (
-            mine[...] + side[...] + across[...] + jnp.where(inner_device(), 0.0, first[...]))
+        out_ref[:, :, start:start + cells] = mine[...] + side[...]
+        start += cells
+    refs = refs[2 * len(NEAR_SPLIT):-1]
+    start = 0
+    for piece in range(len(SPLIT)):
+        first, across = refs[2 * piece:2 * piece + 2]
+        cells = first.shape[-1]
+        out_ref[:, :, start:start + cells] += across[...] + jnp.where(inner_device(), 0.0, first[...])
         start += cells
 
 
@@ -231,26 +256,22 @@
         compiler_params=pltpu.CompilerParams(vmem_limit_bytes=8 << 20))(*args)
 
 
-def four_owners(pair_of, pieces):
-    firsts, acrosses, threes, args = [], [], [], []
-
-    def relay(piece):
-        joined = in_vmem(join_kernel, threes[piece].shape, (threes[piece], firsts[piece]), IN_VMEM)
-        acrosses.append(lax.ppermute(joined, "space", ACROSS))
-        return joined
-
-    after = None
-    for piece in range(pieces):
-        two, three = pair_of(flipped(2, 3), piece, after)
-        firsts.append(lax.ppermute(two, "space", FIRST))
+def four_owners(pair_of):
+    far, near = [], []
+    threes, after = [], None
+    for piece in range(len(SPLIT)):
+        two, three = pair_of(flipped(2, 3), SPLIT, piece, after)
+        far.append([lax.ppermute(two, "space", FIRST)])
         threes.append(three)
         after = two
-    for piece in range(pieces):
-        after = relay(piece)
-        one, mine = pair_of(flipped(1, 0), piece, after)
-        args += [mine, lax.ppermute(one, "space", SIDE), firsts[piece], acrosses[piece]]
-    shape = mine.shape[:2] + (sum(a.shape[-1] for a in args[::4]),)
-    return in_vmem(finish_kernel, shape, args, pl.BlockSpec())
+    for piece in range(len(NEAR_SPLIT)):
+        if piece < len(SPLIT):
+            after = in_vmem(join_kernel, threes[piece].shape, (threes[piece], *far[piece]), IN_VMEM)
+            far[piece].append(lax.ppermute(after, "space", ACROSS))
+        one, mine = pair_of(flipped(1, 0), NEAR_SPLIT, piece, after)
+        near.append([mine, lax.ppermute(one, "space", SIDE)])
+    args = [a for pair in near + far for a in pair]
+    return in_vmem(finish_kernel, mine.shape[:2] + (GX * GX,), args, pl.BlockSpec())
 
 
 def local(intensity, image_grad, owner, coord_xy, coord_z):
@@ -262,8 +283,8 @@
     raw = [intensity, image_grad, owner.reshape(1, samples), coord_z.reshape(1, samples)]
     prepared = []
 
-    def pair_of(owners, piece, after=None):
-        first_x, width = sum(SPLIT[:piece]), SPLIT[piece]
+    def pair_of(owners, split, piece, after=None):
+        first_x, width = sum(split[:piece]), split[piece]
         after = stats[0] if after is None else after
         if prepared:
             return pair_grid(owners, [*prepared, *weights], first_x, width, after)[0]
@@ -272,13 +293,13 @@
         return outs
 
     if size == 4:
-        grid = four_owners(pair_of, len(SPLIT))
+        grid = four_owners(pair_of)
     else:
         columns = []
         for piece in range(len(SPLIT)):
             chunks = []
             for start in range(0, size, 2):
-                chunks += pair_of(lambda start=start: (start, min(start + 1, size - 1)), piece)
+                chunks += pair_of(lambda start=start: (start, min(start + 1, size - 1)), SPLIT, piece)
             table = jnp.stack(chunks)
             columns.append(chain(lambda j: lax.dynamic_index_in_dim(
                 table, jnp.clip(j, 0, size - 1), 0, keepdims=False)))

time: 54.2 us -> 49.9 us (0.921)
  Pallas kernels: 27.4 us -> 22.6 us
  starting transfers between devices: 10.4 us -> 12.6 us
  waiting for transfers between devices: 15.2 us -> 13.5 us
    pallas_call x4, Pallas kernels: 24 us -> 19.2 us  [pair_grid(): pl.pallas_call(functools.partial(pair_kernel, n_stats=len(stats), owners=...]
    ppermute x9, starting transfers between devices: 10.4 us -> 12.6 us  [the longest x2 4.7 us: four_owners(): far.append([lax.ppermute(two, 'space', FIRST)])]
    ppermute x9, waiting for transfers between devices: 15.2 us -> 13.5 us  [the longest x2 8.11 us: four_owners(): near.append([mine, lax.ppermute(one, 'space', SIDE)])]
  transfers between devices with their start and end apart: 9 -> 9, of which waited for: 4 -> 3; matrix products, arithmetic and copies ran while one was open for 0% -> 0% of each run, Pallas kernels for 37% -> 33%
where the time goes in v3:
time: 49.9 us; the launch traced here: 49.8 us
  Pallas kernels  22.6 us (45%)
  waiting for transfers between devices  13.5 us (27%)
  starting transfers between devices  12.6 us (25%)
  local copies, waits for them, and re-layouts  0.98 us (2%)
    pallas_call x4, Pallas kernels, pair_grid(): pl.pallas_call(functools.partial(pair_kernel, n_stats=len(stats), owners=...  19.2 us
    ppermute x2, waiting for transfers between devices, four_owners(): near.append([mine, lax.ppermute(one, 'space', SIDE)])  8.11 us
    ppermute x2, starting transfers between devices, four_owners(): far.append([lax.ppermute(two, 'space', FIRST)])  4.7 us
    ppermute x1, waiting for transfers between devices, from_other_phases(): chip = lax.ppermute(stats, 'phase', [(i, i ^ 2) for i in range(size)])  3.49 us
    ppermute x1, starting transfers between devices, from_other_phases(): chip = lax.ppermute(stats, 'phase', [(i, i ^ 2) for i in range(size)])  3.03 us
    ppermute x2, starting transfers between devices, four_owners(): far[piece].append(lax.ppermute(after, 'space', ACROSS))  2.73 us
    pallas_call x1, Pallas kernels, plane_weights(): pl.pallas_call(weights_kernel, out_shape=[jax.ShapeDtypeStruct((GX, sampl...  2.16 us
    ppermute x2, starting transfers between devices, four_owners(): near.append([mine, lax.ppermute(one, 'space', SIDE)])  2.13 us
  transfers between devices with their start and end apart: 9, of which 3 were waited for; matrix products, arithmetic and copies ran while one was open for 0% of the time, Pallas kernels for 33%

profile of v3, /device:TPU:0, one launch (start us, length us, event | category | flops | bytes accessed | tf_op | source)
XLA Modules:
  0.0 49.8 jit_solution(12324794884925538191)
XLA Ops:
  0.0 0.0 copy-start.1
  0.0 0.9 %copy-done.1 = f32[4,16384]{1,0:T(4,128)S(1)} copy-done((f32[4,16384]{1,0:T(4,128)S(1)}, f32[4,16384]{1,0:T(4,128)}, u32[]{:S(2)}) %copy-start.1) | copy-done | bytes 262168
  1.0 0.0 copy-start.5
  1.0 0.4 phase_stats.1.refs_4_.refs_10_
  1.3 0.0 copy-start
  1.3 0.0 copy-start.2
  1.3 0.0 copy-start.3
  1.3 0.0 copy-start.4
  1.4 3.0 %collective-permute-start.1 = (f32[2,16384]{1,0:T(2,128)S(1)}, f32[2,16384]{1,0:T(2,128)S(1)}, u32[]{:S(2)}, u32[]{:S(2)}) collective-permute-start(f32[2,16384]{1,0:T(2,128)S(1)} %phase_stats.1.refs_4_.refs_10_), channel_id=1, source_target_pairs={{0,2},{1,3},{2,0},{3,1},{4,6},{5,7},{6,4},{7,5},{8,10},{9,11},{10,... | collective-permute-start | bytes 393224 | tf_op jit(solution)/shard_map/ppermute | solution.py:191
  4.4 0.0 collective-permute-start
  4.4 3.5 %collective-permute-done.1.refs_6_ = f32[2,16384]{1,0:T(2,128)S(1)} collective-permute-done((f32[2,16384]{1,0:T(2,128)S(1)}, f32[2,16384]{1,0:T(2,128)S(1)}, u32[]{:S(2)}, u32[]{:S(2)}) %collective-permute-start.1) | collective-permute-done | bytes 131104 | tf_op jit(solution)/shard_map/ppermute | solution.py:191
  7.9 0.0 collective-permute-start.2
  7.9 0.0 copy-done.5
  7.9 2.2 %plane_weights.1 = (f32[32,16384]{1,0:T(8,128)S(1)}, f32[32,16384]{1,0:T(8,128)S(1)}) custom-call(s32[2,16384]{1,0:T(2,128)S(1)} %copy-done.5), custom_call_target="tpu_custom_call" | custom-call | flops 1073741824 | bytes 12582912 | tf_op jit(solution)/shard_map/plane_weights/pallas_call | solution.py:64
  10.1 0.0 collective-permute-done.refs_5_
  10.1 0.0 collective-permute-done.2.refs_7_
  10.1 0.0 copy-done
  10.1 0.0 copy-done.2
  10.1 0.0 copy-done.3
  10.1 0.0 copy-done.4
  10.1 4.9 %pair_grid.4 = (f32[96,512]{1,0:T(8,128)S(1)}, f32[96,512]{1,0:T(8,128)S(1)}, f32[12,16384]{1,0:T(8,128)S(1)}, f32[1,16384]{1,0:T(1,128)S(1)}) custom-call(f32[4,16384]{1,0:T(4,128)S(1)} %copy-done.2, bf16[3,4,16384]{2,1,0:T(4,128)(2,1)S(1)} %copy-done, s32[1,16384]{1,0:T(1,128)S(1)} %bitcast.17, s32[1,16384]{1,0:T(1,128)S(1)} %bitcast.18, ...), custom_call_target="tpu_custom_call" | custom-call | flops 1073741824 | bytes 12582912 | tf_op jit(solution)/shard_map/pair_grid/pallas_call | solution.py:169
  15.0 1.9 %collective-permute-start.3 = (f32[12,8,512]{2,1,0:T(8,128)S(1)}, f32[12,8,512]{2,1,0:T(8,128)S(1)}, u32[]{:S(2)}, u32[]{:S(2)}) collective-permute-start(f32[12,8,512]{2,1,0:T(8,128)S(1)} %bitcast.12), channel_id=1, source_target_pairs={{0,4},{4,12},{12,8},{8,0},{1,5},{5,13},{13,9},{9,1},{2,6},{6,14},{... | collective-permute-start | bytes 589832 | tf_op jit(solution)/shard_map/ppermute | solution.py:264
  16.9 4.8 %pair_grid.6 = (f32[96,512]{1,0:T(8,128)S(1)}, f32[96,512]{1,0:T(8,128)S(1)}) custom-call(f32[12,16384]{1,0:T(8,128)S(1)} %get-tuple-element.19.refs_0_, f32[1,16384]{1,0:T(1,128)S(1)} %get-tuple-element.20.refs_1_, f32[32,16384]{1,0:T(8,128)S(1)} %get-tuple-element.17.refs_8_.refs_2_, f32[32,16384]{1,0:T(8,128)S(1)} %get-tuple-element.18.refs_9_.refs_3_, ...), custom_call_target="tpu_custom_call" | custom-call | flops 1073741824 | bytes 12582912 | tf_op jit(solution)/shard_map/pair_grid/pallas_call | solution.py:169
  21.7 2.8 %collective-permute-start.5 = (f32[12,8,512]{2,1,0:T(8,128)S(1)}, f32[12,8,512]{2,1,0:T(8,128)S(1)}, u32[]{:S(2)}, u32[]{:S(2)}) collective-permute-start(f32[12,8,512]{2,1,0:T(8,128)S(1)} %bitcast.20), channel_id=1, source_target_pairs={{0,4},{4,12},{12,8},{8,0},{1,5},{5,13},{13,9},{9,1},{2,6},{6,14},{... | collective-permute-start | bytes 589832 | tf_op jit(solution)/shard_map/ppermute | solution.py:264
  24.5 0.0 collective-permute-done.3.got_ref.refs_4_
  24.6 2.7 %collective-permute-start.7 = (f32[12,8,512]{2,1,0:T(8,128)S(1)}, f32[12,8,512]{2,1,0:T(8,128)S(1)}, u32[]{:S(2)}, u32[]{:S(2)}) collective-permute-start(f32[12,8,512]{2,1,0:T(8,128)S(1)} %shard_map.55.refs_4_), channel_id=1, source_target_pairs={{0,12},{12,0},{4,8},{8,4},{1,13},{13,1},{5,9},{9,5},{2,14},{14,2},... | collective-permute-start | bytes 589832 | tf_op jit(solution)/shard_map/ppermute | solution.py:270
  27.2 5.8 %pair_grid.5 = (f32[96,640]{1,0:T(8,128)S(1)}, f32[96,640]{1,0:T(8,128)S(1)}) custom-call(f32[12,16384]{1,0:T(8,128)S(1)} %get-tuple-element.19.refs_0_, f32[1,16384]{1,0:T(1,128)S(1)} %get-tuple-element.20.refs_1_, f32[32,16384]{1,0:T(8,128)S(1)} %get-tuple-element.17.refs_8_.refs_2_, f32[32,16384]{1,0:T(8,128)S(1)} %get-tuple-element.18.refs_9_.refs_3_, ...), custom_call_target="tpu_custom_call" | custom-call | flops 1073741824 | bytes 12582912 | tf_op jit(solution)/shard_map/pair_grid/pallas_call | solution.py:169
  33.0 1.8 %collective-permute-done.5.got_ref.refs_6_ = f32[12,8,512]{2,1,0:T(8,128)S(1)} collective-permute-done((f32[12,8,512]{2,1,0:T(8,128)S(1)}, f32[12,8,512]{2,1,0:T(8,128)S(1)}, u32[]{:S(2)}, u32[]{:S(2)}) %collective-permute-start.5) | collective-permute-done | bytes 196640 | tf_op jit(solution)/shard_map/ppermute | solution.py:264
  34.9 0.1 collective-permute-start.8
  34.9 0.1 collective-permute-start.4
  35.0 3.8 %pair_grid.7 = (f32[96,384]{1,0:T(8,128)S(1)}, f32[96,384]{1,0:T(8,128)S(1)}) custom-call(f32[12,16384]{1,0:T(8,128)S(1)} %get-tuple-element.19.refs_0_, f32[1,16384]{1,0:T(1,128)S(1)} %get-tuple-element.20.refs_1_, f32[32,16384]{1,0:T(8,128)S(1)} %get-tuple-element.17.refs_8_.refs_2_, f32[32,16384]{1,0:T(8,128)S(1)} %get-tuple-element.18.refs_9_.refs_3_, ...), custom_call_target="tpu_custom_call" | custom-call | flops 1073741824 | bytes 12582912 | tf_op jit(solution)/shard_map/pair_grid/pallas_call | solution.py:169
  38.8 2.1 %collective-permute-start.6 = (f32[12,8,384]{2,1,0:T(8,128)S(1)}, f32[12,8,384]{2,1,0:T(8,128)S(1)}, u32[]{:S(2)}, u32[]{:S(2)}) collective-permute-start(f32[12,8,384]{2,1,0:T(8,128)S(1)} %bitcast.21), channel_id=1, source_target_pairs={{0,4},{4,0},{8,12},{12,8},{1,5},{5,1},{9,13},{13,9},{2,6},{6,2},{1... | collective-permute-start | bytes 442376 | tf_op jit(solution)/shard_map/ppermute | solution.py:272
  40.8 8.1 %collective-permute-done.6.refs_3_ = f32[12,8,384]{2,1,0:T(8,128)S(1)} collective-permute-done((f32[12,8,384]{2,1,0:T(8,128)S(1)}, f32[12,8,384]{2,1,0:T(8,128)S(1)}, u32[]{:S(2)}, u32[]{:S(2)}) %collective-permute-start.6) | collective-permute-done | bytes 147488 | tf_op jit(solution)/shard_map/ppermute | solution.py:272
  49.0 0.0 collective-permute-done.8.refs_7_
  49.0 0.0 collective-permute-done.7.refs_5_
  49.0 0.0 collective-permute-done.4.refs_1_
  49.0 0.8 %shard_map.57 = f32[12,8,1024]{2,1,0:T(8,128)} custom-call(f32[12,8,640]{2,1,0:T(8,128)S(1)} %bitcast.11, f32[12,8,640]{2,1,0:T(8,128)S(1)} %collective-permute-done.4.refs_1_, f32[12,8,384]{2,1,0:T(8,128)S(1)} %bitcast.16, f32[12,8,384]{2,1,0:T(8,128)S(1)} %collective-permute-done.6.refs_3_, f32[12,8,512]{2,1,0:T(8,128)S(1)} %collective-permute-done.3.got_ref.refs_4_, ...), custom_call_target="tpu_custom_call" | custom-call | tf_op jit(solution)/shard_map/pallas_call | solution.py:253
  (2 shorter events, 0.1 us)
Async XLA Ops:
  0.0 0.9 %copy-start.1 = (f32[4,16384]{1,0:T(4,128)S(1)}, f32[4,16384]{1,0:T(4,128)}, u32[]{:S(2)}) copy-start(f32[4,16384]{1,0:T(4,128)} %refs_0_.1) | copy-start | bytes 786436
  1.0 6.9 %copy-start.5 = (s32[2,16384]{1,0:T(2,128)S(1)}, s32[2,16384]{1,0:T(2,128)}, u32[]{:S(2)}) copy-start(s32[2,16384]{1,0:T(2,128)} %coord_ref.1) | copy-start | bytes 393220
  1.3 8.8 %copy-start = (bf16[3,4,16384]{2,1,0:T(4,128)(2,1)S(1)}, bf16[3,4,16384]{2,1,0:T(4,128)(2,1)}, u32[]{:S(2)}) copy-start(bf16[3,4,16384]{2,1,0:T(4,128)(2,1)} %refs_1_.1) | copy-start | bytes 1179652
  1.3 8.8 %copy-start.2 = (f32[4,16384]{1,0:T(4,128)S(1)}, f32[4,16384]{1,0:T(4,128)}, u32[]{:S(2)}) copy-start(f32[4,16384]{1,0:T(4,128)} %refs_0_.1) | copy-start | bytes 786436
  1.3 8.8 %copy-start.3 = (s32[16384,1]{0,1:T(1,128)S(1)}, s32[16384,1]{0,1:T(1,128)}, u32[]{:S(2)}) copy-start(s32[16384,1]{0,1:T(1,128)} %param.7) | copy-start | bytes 196612
  1.3 8.8 %copy-start.4 = (s32[16384]{0:T(1024)S(1)}, s32[16384]{0:T(1024)}, u32[]{:S(2)}) copy-start(s32[16384]{0:T(1024)} %param.9) | copy-start | bytes 196612
  1.4 6.5 %collective-permute-start.1 = (f32[2,16384]{1,0:T(2,128)S(1)}, f32[2,16384]{1,0:T(2,128)S(1)}, u32[]{:S(2)}, u32[]{:S(2)}) collective-permute-start(f32[2,16384]{1,0:T(2,128)S(1)} %phase_stats.1.refs_4_.refs_10_), channel_id=1, source_target_pairs={{0,2},{1,3},{2,0},{3,1},{4,6},{5,7},{6,4},{7,5},{8,10},{9,11},{10,... | collective-permute-start | bytes 393224 | tf_op jit(solution)/shard_map/ppermute | solution.py:191
  4.4 5.7 %collective-permute-start = (f32[2,16384]{1,0:T(2,128)S(1)}, f32[2,16384]{1,0:T(2,128)S(1)}, u32[]{:S(2)}, u32[]{:S(2)}) collective-permute-start(f32[2,16384]{1,0:T(2,128)S(1)} %phase_stats.1.refs_4_.refs_10_), channel_id=1, source_target_pairs={{0,1},{1,0},{2,3},{3,2},{4,5},{5,4},{6,7},{7,6},{8,9},{9,8},{10,11... | collective-permute-start | bytes 393224 | tf_op jit(solution)/shard_map/ppermute | solution.py:192
  7.9 2.2 %collective-permute-start.2 = (f32[2,16384]{1,0:T(2,128)S(1)}, f32[2,16384]{1,0:T(2,128)S(1)}, u32[]{:S(2)}, u32[]{:S(2)}) collective-permute-start(f32[2,16384]{1,0:T(2,128)S(1)} %collective-permute-done.1.refs_6_), channel_id=1, source_target_pairs={{0,1},{1,0},{2,3},{3,2},{4,5},{5,4},{6,7},{7,6},{8,9},{9,8},{10,11... | collective-permute-start | bytes 393224 | tf_op jit(solution)/shard_map/ppermute | solution.py:193
  15.0 9.5 %collective-permute-start.3 = (f32[12,8,512]{2,1,0:T(8,128)S(1)}, f32[12,8,512]{2,1,0:T(8,128)S(1)}, u32[]{:S(2)}, u32[]{:S(2)}) collective-permute-start(f32[12,8,512]{2,1,0:T(8,128)S(1)} %bitcast.12), channel_id=1, source_target_pairs={{0,4},{4,12},{12,8},{8,0},{1,5},{5,13},{13,9},{9,1},{2,6},{6,14},{... | collective-permute-start | bytes 589832 | tf_op jit(solution)/shard_map/ppermute | solution.py:264
  21.7 13.1 %collective-permute-start.5 = (f32[12,8,512]{2,1,0:T(8,128)S(1)}, f32[12,8,512]{2,1,0:T(8,128)S(1)}, u32[]{:S(2)}, u32[]{:S(2)}) collective-permute-start(f32[12,8,512]{2,1,0:T(8,128)S(1)} %bitcast.20), channel_id=1, source_target_pairs={{0,4},{4,12},{12,8},{8,0},{1,5},{5,13},{13,9},{9,1},{2,6},{6,14},{... | collective-permute-start | bytes 589832 | tf_op jit(solution)/shard_map/ppermute | solution.py:264
  24.6 24.4 %collective-permute-start.7 = (f32[12,8,512]{2,1,0:T(8,128)S(1)}, f32[12,8,512]{2,1,0:T(8,128)S(1)}, u32[]{:S(2)}, u32[]{:S(2)}) collective-permute-start(f32[12,8,512]{2,1,0:T(8,128)S(1)} %shard_map.55.refs_4_), channel_id=1, source_target_pairs={{0,12},{12,0},{4,8},{8,4},{1,13},{13,1},{5,9},{9,5},{2,14},{14,2},... | collective-permute-start | bytes 589832 | tf_op jit(solution)/shard_map/ppermute | solution.py:270
  34.9 14.1 %collective-permute-start.8 = (f32[12,8,512]{2,1,0:T(8,128)S(1)}, f32[12,8,512]{2,1,0:T(8,128)S(1)}, u32[]{:S(2)}, u32[]{:S(2)}) collective-permute-start(f32[12,8,512]{2,1,0:T(8,128)S(1)} %shard_map.56.refs_4_), channel_id=1, source_target_pairs={{0,12},{12,0},{4,8},{8,4},{1,13},{13,1},{5,9},{9,5},{2,14},{14,2},... | collective-permute-start | bytes 589832 | tf_op jit(solution)/shard_map/ppermute | solution.py:270
  34.9 14.0 %collective-permute-start.4 = (f32[12,8,640]{2,1,0:T(8,128)S(1)}, f32[12,8,640]{2,1,0:T(8,128)S(1)}, u32[]{:S(2)}, u32[]{:S(2)}) collective-permute-start(f32[12,8,640]{2,1,0:T(8,128)S(1)} %bitcast.19), channel_id=1, source_target_pairs={{0,4},{4,0},{8,12},{12,8},{1,5},{5,1},{9,13},{13,9},{2,6},{6,2},{1... | collective-permute-start | bytes 737288 | tf_op jit(solution)/shard_map/ppermute | solution.py:272
  38.8 10.2 %collective-permute-start.6 = (f32[12,8,384]{2,1,0:T(8,128)S(1)}, f32[12,8,384]{2,1,0:T(8,128)S(1)}, u32[]{:S(2)}, u32[]{:S(2)}) collective-permute-start(f32[12,8,384]{2,1,0:T(8,128)S(1)} %bitcast.21), channel_id=1, source_target_pairs={{0,4},{4,0},{8,12},{12,8},{1,5},{5,1},{9,13},{13,9},{2,6},{6,2},{1... | collective-permute-start | bytes 442376 | tf_op jit(solution)/shard_map/ppermute | solution.py:272

commit v4 on v3

--- a/solution.py
+++ b/solution.py
@@ -11,11 +11,11 @@
 GX = 32
 SPC = 16
 GZ_DEV = 8
-BLOCKS = (1024, 2048, 4096, 4608)
+BLOCKS = (1536, 3072, 5632, 6144)
 SUB = 512
 STEP = 512
 SPLIT = (16, 16)
-NEAR_SPLIT = (20, 12)
+NEAR_SPLIT = (16, 16)
 COST = pl.CostEstimate(flops=1 << 30, bytes_accessed=12 << 20, transcendentals=0)
 
 IN_VMEM = pl.BlockSpec(memory_space=pltpu.VMEM)
@@ -146,10 +146,10 @@
             build(block + 1, *buffers[(block + 1) % 2])
         part = multiply(block, *buffers[block % 2])
         if block:
-            total[...] += part
-        else:
+            part = total[...] + part
+        if block + 1 < len(sizes):
             total[...] = part
-    both = total[...].T
+    both = part.T
     first_ref[...] = both[:half]
     second_ref[...] = both[half:]
 
@@ -178,7 +178,7 @@
             pltpu.VMEM((cells, largest), jnp.bfloat16),
             pltpu.VMEM((cells, 2 * half), jnp.float32),
         ],
-        compiler_params=pltpu.CompilerParams(vmem_limit_bytes=24 << 20),
+        compiler_params=pltpu.CompilerParams(vmem_limit_bytes=32 << 20),
         cost_estimate=COST,
         name="pair_grid",
     )(*args, after)

time: 49.9 us -> 50.2 us (level)
  waiting for transfers between devices: 13.5 us -> 14.8 us
  starting transfers between devices: 12.6 us -> 11.4 us
    ppermute x2, starting transfers between devices: 2.13 us -> 0.14 us  [four_owners(): near.append([mine, lax.ppermute(one, 'space', SIDE)])]
    ppermute x2, waiting for transfers between devices: 1.84 us -> 2.71 us  [four_owners(): far.append([lax.ppermute(two, 'space', FIRST)])]
    ppermute x2, starting transfers between devices: 2.73 us -> 3.51 us  [four_owners(): far[piece].append(lax.ppermute(after, 'space', ACROSS))]
    ppermute x2, waiting for transfers between devices: 8.11 us -> 8.64 us  [four_owners(): near.append([mine, lax.ppermute(one, 'space', SIDE)])]
where the time goes in v4:
time: 50.2 us; the launch traced here: 50.1 us
  Pallas kernels  22.7 us (45%)
  waiting for transfers between devices  14.8 us (29%)
  starting transfers between devices  11.4 us (23%)
  local copies, waits for them, and re-layouts  0.98 us (2%)
    pallas_call x4, Pallas kernels, pair_grid(): pl.pallas_call(functools.partial(pair_kernel, n_stats=len(stats), owners=...  19.3 us
    ppermute x2, waiting for transfers between devices, four_owners(): near.append([mine, lax.ppermute(one, 'space', SIDE)])  8.64 us
    ppermute x2, starting transfers between devices, four_owners(): far.append([lax.ppermute(two, 'space', FIRST)])  4.7 us
    ppermute x2, starting transfers between devices, four_owners(): far[piece].append(lax.ppermute(after, 'space', ACROSS))  3.51 us
    ppermute x1, waiting for transfers between devices, from_other_phases(): chip = lax.ppermute(stats, 'phase', [(i, i ^ 2) for i in range(size)])  3.49 us
    ppermute x1, starting transfers between devices, from_other_phases(): chip = lax.ppermute(stats, 'phase', [(i, i ^ 2) for i in range(size)])  3.03 us
    ppermute x2, waiting for transfers between devices, four_owners(): far.append([lax.ppermute(two, 'space', FIRST)])  2.71 us
    pallas_call x1, Pallas kernels, plane_weights(): pl.pallas_call(weights_kernel, out_shape=[jax.ShapeDtypeStruct((GX, sampl...  2.16 us
  transfers between devices with their start and end apart: 9, of which 3 were waited for; matrix products, arithmetic and copies ran while one was open for 0% of the time, Pallas kernels for 33%

profile of v4, /device:TPU:0, one launch (start us, length us, event | category | flops | bytes accessed | tf_op | source)
XLA Modules:
  0.0 50.1 jit_solution(17368215121315095714)
XLA Ops:
  0.0 0.0 copy-start.1
  0.0 0.9 %copy-done.1 = f32[4,16384]{1,0:T(4,128)S(1)} copy-done((f32[4,16384]{1,0:T(4,128)S(1)}, f32[4,16384]{1,0:T(4,128)}, u32[]{:S(2)}) %copy-start.1) | copy-done | bytes 262168
  1.0 0.0 copy-start.5
  1.0 0.4 phase_stats.1.refs_4_.refs_10_
  1.3 0.0 copy-start
  1.3 0.0 copy-start.2
  1.3 0.0 copy-start.3
  1.3 0.0 copy-start.4
  1.4 3.0 %collective-permute-start.1 = (f32[2,16384]{1,0:T(2,128)S(1)}, f32[2,16384]{1,0:T(2,128)S(1)}, u32[]{:S(2)}, u32[]{:S(2)}) collective-permute-start(f32[2,16384]{1,0:T(2,128)S(1)} %phase_stats.1.refs_4_.refs_10_), channel_id=1, source_target_pairs={{0,2},{1,3},{2,0},{3,1},{4,6},{5,7},{6,4},{7,5},{8,10},{9,11},{10,... | collective-permute-start | bytes 393224 | tf_op jit(solution)/shard_map/ppermute | solution.py:191
  4.4 0.0 collective-permute-start
  4.4 3.5 %collective-permute-done.1.refs_6_ = f32[2,16384]{1,0:T(2,128)S(1)} collective-permute-done((f32[2,16384]{1,0:T(2,128)S(1)}, f32[2,16384]{1,0:T(2,128)S(1)}, u32[]{:S(2)}, u32[]{:S(2)}) %collective-permute-start.1) | collective-permute-done | bytes 131104 | tf_op jit(solution)/shard_map/ppermute | solution.py:191
  7.9 0.0 collective-permute-start.2
  7.9 0.0 copy-done.5
  7.9 2.2 %plane_weights.1 = (f32[32,16384]{1,0:T(8,128)S(1)}, f32[32,16384]{1,0:T(8,128)S(1)}) custom-call(s32[2,16384]{1,0:T(2,128)S(1)} %copy-done.5), custom_call_target="tpu_custom_call" | custom-call | flops 1073741824 | bytes 12582912 | tf_op jit(solution)/shard_map/plane_weights/pallas_call | solution.py:64
  10.1 0.0 collective-permute-done.refs_5_
  10.1 0.0 collective-permute-done.2.refs_7_
  10.1 0.0 copy-done
  10.1 0.0 copy-done.2
  10.1 0.0 copy-done.3
  10.1 0.0 copy-done.4
  10.1 4.9 %pair_grid.4 = (f32[96,512]{1,0:T(8,128)S(1)}, f32[96,512]{1,0:T(8,128)S(1)}, f32[12,16384]{1,0:T(8,128)S(1)}, f32[1,16384]{1,0:T(1,128)S(1)}) custom-call(f32[4,16384]{1,0:T(4,128)S(1)} %copy-done.2, bf16[3,4,16384]{2,1,0:T(4,128)(2,1)S(1)} %copy-done, s32[1,16384]{1,0:T(1,128)S(1)} %bitcast.17, s32[1,16384]{1,0:T(1,128)S(1)} %bitcast.18, ...), custom_call_target="tpu_custom_call" | custom-call | flops 1073741824 | bytes 12582912 | tf_op jit(solution)/shard_map/pair_grid/pallas_call | solution.py:169
  15.0 1.9 %collective-permute-start.3 = (f32[12,8,512]{2,1,0:T(8,128)S(1)}, f32[12,8,512]{2,1,0:T(8,128)S(1)}, u32[]{:S(2)}, u32[]{:S(2)}) collective-permute-start(f32[12,8,512]{2,1,0:T(8,128)S(1)} %bitcast.11), channel_id=1, source_target_pairs={{0,4},{4,12},{12,8},{8,0},{1,5},{5,13},{13,9},{9,1},{2,6},{6,14},{... | collective-permute-start | bytes 589832 | tf_op jit(solution)/shard_map/ppermute | solution.py:264
  16.9 4.8 %pair_grid.6 = (f32[96,512]{1,0:T(8,128)S(1)}, f32[96,512]{1,0:T(8,128)S(1)}) custom-call(f32[12,16384]{1,0:T(8,128)S(1)} %get-tuple-element.19.refs_0_, f32[1,16384]{1,0:T(1,128)S(1)} %get-tuple-element.20.refs_1_, f32[32,16384]{1,0:T(8,128)S(1)} %get-tuple-element.17.refs_8_.refs_2_, f32[32,16384]{1,0:T(8,128)S(1)} %get-tuple-element.18.refs_9_.refs_3_, ...), custom_call_target="tpu_custom_call" | custom-call | flops 1073741824 | bytes 12582912 | tf_op jit(solution)/shard_map/pair_grid/pallas_call | solution.py:169
  21.7 2.8 %collective-permute-start.5 = (f32[12,8,512]{2,1,0:T(8,128)S(1)}, f32[12,8,512]{2,1,0:T(8,128)S(1)}, u32[]{:S(2)}, u32[]{:S(2)}) collective-permute-start(f32[12,8,512]{2,1,0:T(8,128)S(1)} %bitcast.20), channel_id=1, source_target_pairs={{0,4},{4,12},{12,8},{8,0},{1,5},{5,13},{13,9},{9,1},{2,6},{6,14},{... | collective-permute-start | bytes 589832 | tf_op jit(solution)/shard_map/ppermute | solution.py:264
  24.5 0.0 collective-permute-done.3.got_ref.refs_4_
  24.6 2.7 %collective-permute-start.7 = (f32[12,8,512]{2,1,0:T(8,128)S(1)}, f32[12,8,512]{2,1,0:T(8,128)S(1)}, u32[]{:S(2)}, u32[]{:S(2)}) collective-permute-start(f32[12,8,512]{2,1,0:T(8,128)S(1)} %shard_map.55.refs_4_), channel_id=1, source_target_pairs={{0,12},{12,0},{4,8},{8,4},{1,13},{13,1},{5,9},{9,5},{2,14},{14,2},... | collective-permute-start | bytes 589832 | tf_op jit(solution)/shard_map/ppermute | solution.py:270
  27.2 4.8 %pair_grid.5 = (f32[96,512]{1,0:T(8,128)S(1)}, f32[96,512]{1,0:T(8,128)S(1)}) custom-call(f32[12,16384]{1,0:T(8,128)S(1)} %get-tuple-element.19.refs_0_, f32[1,16384]{1,0:T(1,128)S(1)} %get-tuple-element.20.refs_1_, f32[32,16384]{1,0:T(8,128)S(1)} %get-tuple-element.17.refs_8_.refs_2_, f32[32,16384]{1,0:T(8,128)S(1)} %get-tuple-element.18.refs_9_.refs_3_, ...), custom_call_target="tpu_custom_call" | custom-call | flops 1073741824 | bytes 12582912 | tf_op jit(solution)/shard_map/pair_grid/pallas_call | solution.py:169
  32.0 0.1 collective-permute-start.4
  32.1 2.7 %collective-permute-done.5.got_ref.refs_6_ = f32[12,8,512]{2,1,0:T(8,128)S(1)} collective-permute-done((f32[12,8,512]{2,1,0:T(8,128)S(1)}, f32[12,8,512]{2,1,0:T(8,128)S(1)}, u32[]{:S(2)}, u32[]{:S(2)}) %collective-permute-start.5) | collective-permute-done | bytes 196640 | tf_op jit(solution)/shard_map/ppermute | solution.py:264
  34.9 4.8 %pair_grid.7 = (f32[96,512]{1,0:T(8,128)S(1)}, f32[96,512]{1,0:T(8,128)S(1)}) custom-call(f32[12,16384]{1,0:T(8,128)S(1)} %get-tuple-element.19.refs_0_, f32[1,16384]{1,0:T(1,128)S(1)} %get-tuple-element.20.refs_1_, f32[32,16384]{1,0:T(8,128)S(1)} %get-tuple-element.17.refs_8_.refs_2_, f32[32,16384]{1,0:T(8,128)S(1)} %get-tuple-element.18.refs_9_.refs_3_, ...), custom_call_target="tpu_custom_call" | custom-call | flops 1073741824 | bytes 12582912 | tf_op jit(solution)/shard_map/pair_grid/pallas_call | solution.py:169
  39.7 0.1 collective-permute-start.6
  39.8 0.8 %collective-permute-start.8 = (f32[12,8,512]{2,1,0:T(8,128)S(1)}, f32[12,8,512]{2,1,0:T(8,128)S(1)}, u32[]{:S(2)}, u32[]{:S(2)}) collective-permute-start(f32[12,8,512]{2,1,0:T(8,128)S(1)} %shard_map.56.refs_4_), channel_id=1, source_target_pairs={{0,12},{12,0},{4,8},{8,4},{1,13},{13,1},{5,9},{9,5},{2,14},{14,2},... | collective-permute-start | bytes 589832 | tf_op jit(solution)/shard_map/ppermute | solution.py:270
  40.6 0.0 collective-permute-done.7.refs_5_
  40.6 0.0 collective-permute-done.4.refs_1_
  40.6 8.6 %collective-permute-done.6.refs_3_ = f32[12,8,512]{2,1,0:T(8,128)S(1)} collective-permute-done((f32[12,8,512]{2,1,0:T(8,128)S(1)}, f32[12,8,512]{2,1,0:T(8,128)S(1)}, u32[]{:S(2)}, u32[]{:S(2)}) %collective-permute-start.6) | collective-permute-done | bytes 196640 | tf_op jit(solution)/shard_map/ppermute | solution.py:272
  49.2 0.0 collective-permute-done.8.refs_7_
  49.3 0.8 %shard_map.57 = f32[12,8,1024]{2,1,0:T(8,128)} custom-call(f32[12,8,512]{2,1,0:T(8,128)S(1)} %bitcast.15, f32[12,8,512]{2,1,0:T(8,128)S(1)} %collective-permute-done.4.refs_1_, f32[12,8,512]{2,1,0:T(8,128)S(1)} %bitcast.16, f32[12,8,512]{2,1,0:T(8,128)S(1)} %collective-permute-done.6.refs_3_, f32[12,8,512]{2,1,0:T(8,128)S(1)} %collective-permute-done.3.got_ref.refs_4_, ...), custom_call_target="tpu_custom_call" | custom-call | tf_op jit(solution)/shard_map/pallas_call | solution.py:253
  (2 shorter events, 0.1 us)
Async XLA Ops:
  0.0 0.9 %copy-start.1 = (f32[4,16384]{1,0:T(4,128)S(1)}, f32[4,16384]{1,0:T(4,128)}, u32[]{:S(2)}) copy-start(f32[4,16384]{1,0:T(4,128)} %refs_0_.1) | copy-start | bytes 786436
  1.0 6.9 %copy-start.5 = (s32[2,16384]{1,0:T(2,128)S(1)}, s32[2,16384]{1,0:T(2,128)}, u32[]{:S(2)}) copy-start(s32[2,16384]{1,0:T(2,128)} %coord_ref.1) | copy-start | bytes 393220
  1.3 8.8 %copy-start = (bf16[3,4,16384]{2,1,0:T(4,128)(2,1)S(1)}, bf16[3,4,16384]{2,1,0:T(4,128)(2,1)}, u32[]{:S(2)}) copy-start(bf16[3,4,16384]{2,1,0:T(4,128)(2,1)} %refs_1_.1) | copy-start | bytes 1179652
  1.3 8.8 %copy-start.2 = (f32[4,16384]{1,0:T(4,128)S(1)}, f32[4,16384]{1,0:T(4,128)}, u32[]{:S(2)}) copy-start(f32[4,16384]{1,0:T(4,128)} %refs_0_.1) | copy-start | bytes 786436
  1.3 8.8 %copy-start.3 = (s32[16384,1]{0,1:T(1,128)S(1)}, s32[16384,1]{0,1:T(1,128)}, u32[]{:S(2)}) copy-start(s32[16384,1]{0,1:T(1,128)} %param.7) | copy-start | bytes 196612
  1.3 8.8 %copy-start.4 = (s32[16384]{0:T(1024)S(1)}, s32[16384]{0:T(1024)}, u32[]{:S(2)}) copy-start(s32[16384]{0:T(1024)} %param.9) | copy-start | bytes 196612
  1.4 6.5 %collective-permute-start.1 = (f32[2,16384]{1,0:T(2,128)S(1)}, f32[2,16384]{1,0:T(2,128)S(1)}, u32[]{:S(2)}, u32[]{:S(2)}) collective-permute-start(f32[2,16384]{1,0:T(2,128)S(1)} %phase_stats.1.refs_4_.refs_10_), channel_id=1, source_target_pairs={{0,2},{1,3},{2,0},{3,1},{4,6},{5,7},{6,4},{7,5},{8,10},{9,11},{10,... | collective-permute-start | bytes 393224 | tf_op jit(solution)/shard_map/ppermute | solution.py:191
  4.4 5.7 %collective-permute-start = (f32[2,16384]{1,0:T(2,128)S(1)}, f32[2,16384]{1,0:T(2,128)S(1)}, u32[]{:S(2)}, u32[]{:S(2)}) collective-permute-start(f32[2,16384]{1,0:T(2,128)S(1)} %phase_stats.1.refs_4_.refs_10_), channel_id=1, source_target_pairs={{0,1},{1,0},{2,3},{3,2},{4,5},{5,4},{6,7},{7,6},{8,9},{9,8},{10,11... | collective-permute-start | bytes 393224 | tf_op jit(solution)/shard_map/ppermute | solution.py:192
  7.9 2.2 %collective-permute-start.2 = (f32[2,16384]{1,0:T(2,128)S(1)}, f32[2,16384]{1,0:T(2,128)S(1)}, u32[]{:S(2)}, u32[]{:S(2)}) collective-permute-start(f32[2,16384]{1,0:T(2,128)S(1)} %collective-permute-done.1.refs_6_), channel_id=1, source_target_pairs={{0,1},{1,0},{2,3},{3,2},{4,5},{5,4},{6,7},{7,6},{8,9},{9,8},{10,11... | collective-permute-start | bytes 393224 | tf_op jit(solution)/shard_map/ppermute | solution.py:193
  15.0 9.5 %collective-permute-start.3 = (f32[12,8,512]{2,1,0:T(8,128)S(1)}, f32[12,8,512]{2,1,0:T(8,128)S(1)}, u32[]{:S(2)}, u32[]{:S(2)}) collective-permute-start(f32[12,8,512]{2,1,0:T(8,128)S(1)} %bitcast.11), channel_id=1, source_target_pairs={{0,4},{4,12},{12,8},{8,0},{1,5},{5,13},{13,9},{9,1},{2,6},{6,14},{... | collective-permute-start | bytes 589832 | tf_op jit(solution)/shard_map/ppermute | solution.py:264
  21.7 13.1 %collective-permute-start.5 = (f32[12,8,512]{2,1,0:T(8,128)S(1)}, f32[12,8,512]{2,1,0:T(8,128)S(1)}, u32[]{:S(2)}, u32[]{:S(2)}) collective-permute-start(f32[12,8,512]{2,1,0:T(8,128)S(1)} %bitcast.20), channel_id=1, source_target_pairs={{0,4},{4,12},{12,8},{8,0},{1,5},{5,13},{13,9},{9,1},{2,6},{6,14},{... | collective-permute-start | bytes 589832 | tf_op jit(solution)/shard_map/ppermute | solution.py:264
  24.6 16.0 %collective-permute-start.7 = (f32[12,8,512]{2,1,0:T(8,128)S(1)}, f32[12,8,512]{2,1,0:T(8,128)S(1)}, u32[]{:S(2)}, u32[]{:S(2)}) collective-permute-start(f32[12,8,512]{2,1,0:T(8,128)S(1)} %shard_map.55.refs_4_), channel_id=1, source_target_pairs={{0,12},{12,0},{4,8},{8,4},{1,13},{13,1},{5,9},{9,5},{2,14},{14,2},... | collective-permute-start | bytes 589832 | tf_op jit(solution)/shard_map/ppermute | solution.py:270
  32.0 8.6 %collective-permute-start.4 = (f32[12,8,512]{2,1,0:T(8,128)S(1)}, f32[12,8,512]{2,1,0:T(8,128)S(1)}, u32[]{:S(2)}, u32[]{:S(2)}) collective-permute-start(f32[12,8,512]{2,1,0:T(8,128)S(1)} %bitcast.19), channel_id=1, source_target_pairs={{0,4},{4,0},{8,12},{12,8},{1,5},{5,1},{9,13},{13,9},{2,6},{6,2},{1... | collective-permute-start | bytes 589832 | tf_op jit(solution)/shard_map/ppermute | solution.py:272
  39.7 9.6 %collective-permute-start.6 = (f32[12,8,512]{2,1,0:T(8,128)S(1)}, f32[12,8,512]{2,1,0:T(8,128)S(1)}, u32[]{:S(2)}, u32[]{:S(2)}) collective-permute-start(f32[12,8,512]{2,1,0:T(8,128)S(1)} %bitcast.21), channel_id=1, source_target_pairs={{0,4},{4,0},{8,12},{12,8},{1,5},{5,1},{9,13},{13,9},{2,6},{6,2},{1... | collective-permute-start | bytes 589832 | tf_op jit(solution)/shard_map/ppermute | solution.py:272
  39.8 9.5 %collective-permute-start.8 = (f32[12,8,512]{2,1,0:T(8,128)S(1)}, f32[12,8,512]{2,1,0:T(8,128)S(1)}, u32[]{:S(2)}, u32[]{:S(2)}) collective-permute-start(f32[12,8,512]{2,1,0:T(8,128)S(1)} %shard_map.56.refs_4_), channel_id=1, source_target_pairs={{0,12},{12,0},{4,8},{8,4},{1,13},{13,1},{5,9},{9,5},{2,14},{14,2},... | collective-permute-start | bytes 589832 | tf_op jit(solution)/shard_map/ppermute | solution.py:270
